TPU v7x, 32 devices: a whole 2x2x4 slice. The times are simulated.
32 devices in a mesh: dp: 16 (over z, y, x), seq: 2 (over core).
Axes of the slice: x: 2, y: 2, z: 4, core: 2. Of those that a mesh axis runs over, the one named last changes fastest.
Arguments:
- inputs: bfloat16 [2, 16, 1024, 1024], P(None, 'dp', 'seq'), may hold values from -6 to 6
- w_query: bfloat16 [1024, 256], P(('dp', 'seq')), may hold values from -0.1875 to 0.1875
- w_key: bfloat16 [1024, 256], P(('dp', 'seq')), may hold values from -0.1875 to 0.1875
- w_value: bfloat16 [1024, 1024], P(('dp', 'seq')), may hold values from -0.1875 to 0.1875
- w_out: bfloat16 [1024, 1024], P(('dp', 'seq')), may hold values from -1 to 1
- w_gate: bfloat16 [1024, 2752], P(('dp', 'seq')), may hold values from -0.1875 to 0.1875
- w_up: bfloat16 [1024, 2752], P(('dp', 'seq')), may hold values from -0.1875 to 0.1875
- w_down: bfloat16 [2752, 1024], P(None, ('dp', 'seq')), may hold values from -0.109375 to 0.109375
- gain_one: bfloat16 [1024], P(('dp', 'seq')), may hold values from 0.25 to 1.75
- gain_two: bfloat16 [1024], P(('dp', 'seq')), may hold values from 0.25 to 1.75
- cotangent: bfloat16 [2, 16, 1024, 1024], P(None, 'dp', 'seq'), may hold values from -6 to 6
Outputs:
- output: bfloat16 [2, 16, 1024, 1024], P(None, 'dp', 'seq')
- input_grad: bfloat16 [2, 16, 1024, 1024], P(None, 'dp', 'seq')
- grad_w_query: float32 [1024, 256], P(('dp', 'seq'))
- grad_w_key: float32 [1024, 256], P(('dp', 'seq'))
- grad_w_value: float32 [1024, 1024], P(('dp', 'seq'))
- grad_w_out: float32 [1024, 1024], P(('dp', 'seq'))
- grad_w_gate: float32 [1024, 2752], P(('dp', 'seq'))
- grad_w_up: float32 [1024, 2752], P(('dp', 'seq'))
- grad_w_down: float32 [2752, 1024], P(None, ('dp', 'seq'))
- grad_gain_one: float32 [1024], P(('dp', 'seq'))
- grad_gain_two: float32 [1024], P(('dp', 'seq'))
All inputs are finite; a program needn't handle non-finite values.
Results may differ from a plain program's by a relative error of at most 0.014.
Values may be sent and summed in bfloat16 or wider, within the bound.
No kernel may reach another device: no remote copies, remote signals or barrier semaphores. Data moves between devices by JAX's collectives and lax.ppermute only.
A program may use at most 320 MiB of HBM per device.

v0:
```python
import jax
import jax.numpy as jnp
from jax import lax
from jax.sharding import PartitionSpec as P

H = 16
F = 16
DV = 64


epsilon = 1e-06
highest_precision = lax.Precision.HIGHEST


def carried_in(value, axis, combine, identity, reverse):
    size, position = (lax.axis_size(axis), lax.axis_index(axis))
    everything = jax.tree.map(lambda part: lax.all_gather(part, axis), value)
    start = jax.tree.map(
        lambda part, zero: jnp.broadcast_to(jnp.asarray(zero, part.dtype), part.shape),
        value,
        identity,
    )

    def lap(k, before):
        at = size - 1 - k if reverse else k
        reached = at > position if reverse else at < position
        new = combine(before, jax.tree.map(lambda part: part[at], everything))
        return jax.tree.map(lambda a, b: jnp.where(reached, a, b), new, before)

    return lax.fori_loop(0, size, lap, start)


def features(vectors):
    feature_width = vectors.shape[-1]
    outer_product = vectors[..., :, None] * vectors[..., None, :]
    outer_product = outer_product.reshape(vectors.shape[:-1] + (feature_width * feature_width,))
    constant = jnp.ones_like(vectors[..., :1])
    return jnp.concatenate(
        [
            constant,
            vectors * feature_width ** (-0.25),
            outer_product * (2.0 * feature_width) ** (-0.5),
        ],
        axis=-1,
    )


def rms_norm(values, gain):
    return values * lax.rsqrt(jnp.mean(values * values, axis=-1, keepdims=True) + epsilon) * gain


def add_pair(earlier, later):
    return (earlier[0] + later[0], earlier[1] + later[1])


def causal_mask(block_rows):
    return jnp.tril(jnp.ones((block_rows, block_rows), jnp.float32))


def kernel_scores(query_sequence, key_sequence):
    attention_score = jnp.einsum(
        "ejx,djx->jed", query_sequence, key_sequence, preferred_element_type=jnp.float32
    ) * query_sequence.shape[-1] ** (-0.5)
    kernel = (1.0 + attention_score + 0.5 * attention_score * attention_score) * causal_mask(
        query_sequence.shape[0]
    )
    return (attention_score, kernel)


def attend_forward(packed):
    query_sequence, key_sequence, value_seq, prior_state, prior_norm = packed
    attention_score, kernel = kernel_scores(query_sequence, key_sequence)
    numerator = jnp.einsum(
        "hqk,khd->qhd", kernel.astype(jnp.bfloat16), value_seq, preferred_element_type=jnp.float32
    )
    denominator = jnp.sum(kernel, axis=-1).T
    query_feats = features(query_sequence.astype(jnp.float32))
    numerator = numerator + jnp.einsum(
        "qhe,hed->qhd", query_feats, prior_state, precision=highest_precision
    )
    denominator = denominator + jnp.einsum(
        "qhe,he->qh", query_feats, prior_norm, precision=highest_precision
    )
    return (numerator / denominator[..., None], denominator)


def attend_backward(packed):
    (
        query_sequence,
        key_sequence,
        value_seq,
        prior_state,
        prior_norm,
        attended,
        denominator,
        grad_attended,
    ) = packed
    attention_score, kernel = kernel_scores(query_sequence, key_sequence)
    kernel_low = kernel.astype(jnp.bfloat16)
    grad_numerator = grad_attended / denominator[..., None]
    grad_denominator = -jnp.sum(grad_attended * attended, axis=-1) / denominator
    grad_numerator_low = grad_numerator.astype(jnp.bfloat16)
    grad_kernel = (
        jnp.einsum(
            "qhd,khd->hqk", grad_numerator_low, value_seq, preferred_element_type=jnp.float32
        )
        + grad_denominator.T[:, :, None]
    )
    score_gradient = (
        grad_kernel * (1.0 + attention_score) * causal_mask(query_sequence.shape[0])
    ).astype(jnp.bfloat16)
    score_scale = query_sequence.shape[-1] ** (-0.5)
    grad_query = (
        jnp.einsum("wpc,cwx->pwx", score_gradient, key_sequence, preferred_element_type=jnp.float32)
        * score_scale
    )
    grad_key = (
        jnp.einsum(
            "crx,rcj->xcj", score_gradient, query_sequence, preferred_element_type=jnp.float32
        )
        * score_scale
    )
    grad_value = jnp.einsum(
        "hqk,qhd->khd", kernel_low, grad_numerator_low, preferred_element_type=jnp.float32
    )
    query_feats, feature_pull = jax.vjp(features, query_sequence.astype(jnp.float32))
    grad_feats = (
        jnp.einsum("qhd,hed->qhe", grad_numerator, prior_state, precision=highest_precision)
        + grad_denominator[..., None] * prior_norm[None]
    )
    grad_query = grad_query + feature_pull(grad_feats)[0]
    grad_prior_state = jnp.einsum(
        "qhe,qhd->hed", query_feats, grad_numerator, precision=highest_precision
    )
    grad_prior_norm = jnp.einsum(
        "qhe,qh->he", query_feats, grad_denominator, precision=highest_precision
    )
    return (grad_query, grad_key, grad_value, grad_prior_state, grad_prior_norm)


def swiglu(gate_input, up_input):
    return jax.nn.silu(gate_input) * up_input


def per_device(
    inputs, w_query, w_key, w_value, w_out, w_gate, w_up, w_down, gain_one, gain_two, cotangent
):
    micro_count, seq_count, block_rows, model_width = inputs.shape
    token_rows = seq_count * block_rows
    gathered = (
        lax.all_gather(w_query, ("dp", "seq"), axis=0, tiled=True),
        lax.all_gather(w_key, ("dp", "seq"), axis=0, tiled=True),
        lax.all_gather(w_value, ("dp", "seq"), axis=0, tiled=True),
        lax.all_gather(w_out, ("dp", "seq"), axis=0, tiled=True),
        lax.all_gather(w_gate, ("dp", "seq"), axis=0, tiled=True),
        lax.all_gather(w_up, ("dp", "seq"), axis=0, tiled=True),
        lax.all_gather(w_down, ("dp", "seq"), axis=1, tiled=True),
        lax.all_gather(gain_one, ("dp", "seq"), axis=0, tiled=True),
        lax.all_gather(gain_two, ("dp", "seq"), axis=0, tiled=True),
    )
    (
        query_full,
        key_full,
        value_full,
        out_full,
        gate_full,
        up_full,
        down_full,
        gain_first,
        gain_second,
    ) = gathered
    gain_first = gain_first.astype(jnp.float32)
    gain_second = gain_second.astype(jnp.float32)
    totals = [jnp.zeros(weight.shape, jnp.float32) for weight in gathered]
    outputs = []
    input_grads = []
    for micro_index in range(micro_count):
        inputs_wide = inputs[micro_index].reshape(token_rows, model_width).astype(jnp.float32)
        normed, norm_one_pull = jax.vjp(rms_norm, inputs_wide, gain_first)
        normed_low = normed.astype(jnp.bfloat16)
        query = jnp.dot(normed_low, query_full, preferred_element_type=jnp.float32).astype(
            jnp.bfloat16
        )
        keys = jnp.dot(normed_low, key_full, preferred_element_type=jnp.float32).astype(
            jnp.bfloat16
        )
        value_proj = jnp.dot(normed_low, value_full, preferred_element_type=jnp.float32).astype(
            jnp.bfloat16
        )
        query_seqs = query.reshape(seq_count, block_rows, H, F)
        key_seqs = keys.reshape(seq_count, block_rows, H, F)
        value_seqs = value_proj.reshape(seq_count, block_rows, H, DV)
        value_wide = value_seqs.astype(jnp.float32)
        key_feats, key_pull = jax.vjp(features, key_seqs.astype(jnp.float32))
        state_s = jnp.einsum("bkhe,bkhd->bhed", key_feats, value_wide, precision=highest_precision)
        state_z = jnp.sum(key_feats, axis=1)
        prior_state, prior_norm = carried_in(
            (state_s, state_z),
            "seq",
            add_pair,
            (jnp.zeros_like(state_s), jnp.zeros_like(state_z)),
            False,
        )
        attended, denominator = lax.map(
            attend_forward, (query_seqs, key_seqs, value_seqs, prior_state, prior_norm)
        )
        attended_low = attended.reshape(token_rows, H * DV).astype(jnp.bfloat16)
        residual = inputs_wide + jnp.dot(attended_low, out_full, preferred_element_type=jnp.float32)
        normed_two, norm_two_pull = jax.vjp(rms_norm, residual, gain_second)
        normed_two_low = normed_two.astype(jnp.bfloat16)
        gate_proj = jnp.dot(normed_two_low, gate_full, preferred_element_type=jnp.float32)
        up_proj = jnp.dot(normed_two_low, up_full, preferred_element_type=jnp.float32)
        hidden_act, swiglu_pull = jax.vjp(swiglu, gate_proj, up_proj)
        hidden_low = hidden_act.astype(jnp.bfloat16)
        result = residual + jnp.dot(hidden_low, down_full, preferred_element_type=jnp.float32)
        outputs.append(result.astype(jnp.bfloat16).reshape(seq_count, block_rows, model_width))
        upstream = cotangent[micro_index].reshape(token_rows, model_width)
        totals[6] = totals[6] + jnp.einsum(
            "tf,td->fd", hidden_low, upstream, preferred_element_type=jnp.float32
        )
        grad_hidden = jnp.einsum(
            "td,fd->tf", upstream, down_full, preferred_element_type=jnp.float32
        )
        grad_gate, grad_up = swiglu_pull(grad_hidden)
        grad_gate_low = grad_gate.astype(jnp.bfloat16)
        grad_up_low = grad_up.astype(jnp.bfloat16)
        totals[4] = totals[4] + jnp.einsum(
            "td,tf->df", normed_two_low, grad_gate_low, preferred_element_type=jnp.float32
        )
        totals[5] = totals[5] + jnp.einsum(
            "td,tf->df", normed_two_low, grad_up_low, preferred_element_type=jnp.float32
        )
        grad_normed_two = jnp.einsum(
            "tf,df->td", grad_gate_low, gate_full, preferred_element_type=jnp.float32
        ) + jnp.einsum("tf,df->td", grad_up_low, up_full, preferred_element_type=jnp.float32)
        grad_residual_norm, grad_gain_second = norm_two_pull(grad_normed_two)
        totals[8] = totals[8] + grad_gain_second
        grad_residual = upstream.astype(jnp.float32) + grad_residual_norm
        grad_mixed_low = grad_residual.astype(jnp.bfloat16)
        totals[3] = totals[3] + jnp.einsum(
            "tc,td->cd", attended_low, grad_mixed_low, preferred_element_type=jnp.float32
        )
        grad_attended = jnp.einsum(
            "td,cd->tc", grad_mixed_low, out_full, preferred_element_type=jnp.float32
        ).reshape(seq_count, block_rows, H, DV)
        grad_query, grad_key, grad_value, grad_prior_state, grad_prior_norm = lax.map(
            attend_backward,
            (
                query_seqs,
                key_seqs,
                value_seqs,
                prior_state,
                prior_norm,
                attended,
                denominator,
                grad_attended,
            ),
        )
        later_state, later_norm = carried_in(
            (grad_prior_state, grad_prior_norm),
            "seq",
            add_pair,
            (jnp.zeros_like(grad_prior_state), jnp.zeros_like(grad_prior_norm)),
            True,
        )
        grad_key_feats = (
            jnp.einsum("bkhd,bhed->bkhe", value_wide, later_state, precision=highest_precision)
            + later_norm[:, None]
        )
        grad_key = grad_key + key_pull(grad_key_feats)[0]
        grad_value = grad_value + jnp.einsum(
            "bkhe,bhed->bkhd", key_feats, later_state, precision=highest_precision
        )
        grad_query_low = grad_query.reshape(token_rows, H * F).astype(jnp.bfloat16)
        grad_key_low = grad_key.reshape(token_rows, H * F).astype(jnp.bfloat16)
        grad_value_low = grad_value.reshape(token_rows, H * DV).astype(jnp.bfloat16)
        totals[0] = totals[0] + jnp.einsum(
            "td,te->de", normed_low, grad_query_low, preferred_element_type=jnp.float32
        )
        totals[1] = totals[1] + jnp.einsum(
            "td,te->de", normed_low, grad_key_low, preferred_element_type=jnp.float32
        )
        totals[2] = totals[2] + jnp.einsum(
            "td,te->de", normed_low, grad_value_low, preferred_element_type=jnp.float32
        )
        grad_normed = jnp.einsum(
            "te,de->td", grad_query_low, query_full, preferred_element_type=jnp.float32
        )
        grad_normed = grad_normed + jnp.einsum(
            "te,de->td", grad_key_low, key_full, preferred_element_type=jnp.float32
        )
        grad_normed = grad_normed + jnp.einsum(
            "te,de->td", grad_value_low, value_full, preferred_element_type=jnp.float32
        )
        grad_inputs_norm, grad_gain_first = norm_one_pull(grad_normed)
        totals[7] = totals[7] + grad_gain_first
        input_grads.append(
            (grad_residual + grad_inputs_norm)
            .astype(jnp.bfloat16)
            .reshape(seq_count, block_rows, model_width)
        )
    shards = (
        lax.psum_scatter(totals[0], ("dp", "seq"), scatter_dimension=0, tiled=True),
        lax.psum_scatter(totals[1], ("dp", "seq"), scatter_dimension=0, tiled=True),
        lax.psum_scatter(totals[2], ("dp", "seq"), scatter_dimension=0, tiled=True),
        lax.psum_scatter(totals[3], ("dp", "seq"), scatter_dimension=0, tiled=True),
        lax.psum_scatter(totals[4], ("dp", "seq"), scatter_dimension=0, tiled=True),
        lax.psum_scatter(totals[5], ("dp", "seq"), scatter_dimension=0, tiled=True),
        lax.psum_scatter(totals[6], ("dp", "seq"), scatter_dimension=1, tiled=True),
        lax.psum_scatter(totals[7], ("dp", "seq"), scatter_dimension=0, tiled=True),
        lax.psum_scatter(totals[8], ("dp", "seq"), scatter_dimension=0, tiled=True),
    )
    return (
        jnp.stack(outputs),
        jnp.stack(input_grads),
        shards[0],
        shards[1],
        shards[2],
        shards[3],
        shards[4],
        shards[5],
        shards[6],
        shards[7],
        shards[8],
    )


def solution(mesh):
    in_specs = (
        P(None, "dp", "seq", None),
        P(("dp", "seq"), None),
        P(("dp", "seq"), None),
        P(("dp", "seq"), None),
        P(("dp", "seq"), None),
        P(("dp", "seq"), None),
        P(("dp", "seq"), None),
        P(None, ("dp", "seq")),
        P(("dp", "seq")),
        P(("dp", "seq")),
        P(None, "dp", "seq", None),
    )
    out_specs = (
        P(None, "dp", "seq", None),
        P(None, "dp", "seq", None),
        P(("dp", "seq"), None),
        P(("dp", "seq"), None),
        P(("dp", "seq"), None),
        P(("dp", "seq"), None),
        P(("dp", "seq"), None),
        P(("dp", "seq"), None),
        P(None, ("dp", "seq")),
        P(("dp", "seq")),
        P(("dp", "seq")),
    )
    return jax.shard_map(
        per_device, mesh=mesh, in_specs=in_specs, out_specs=out_specs, check_vma=False
    )
```

profile of v0, /device:TPU:0, one launch (start us, length us, event | category | flops | bytes accessed | tf_op | source)
XLA Modules:
  0.0 1629.3 jit_solution(9839599318280517353)
XLA Ops:
  9.7 42.0 %all-reduce.5 = (bf16[1024]{0:T(1024)(128)(2,1)S(1)}, bf16[1024]{0:T(1024)(128)(2,1)S(1)}) all-reduce(bf16[1024]{0:T(1024)(128)(2,1)S(1)} %dynamic-update-slice, bf16[1024]{0:T(1024)(128)(2,1)S(1)} %dynamic-update-slice.1), channel_id=1, replica_groups=mesh['dp'=16,'seq'=2] {'dp','seq'}, use_global_device_ids=true, to_apply=%add | all-reduce | flops 2048 | bytes 8192
  53.8 42.0 %all_gather.78 = bf16[1024,256]{1,0:T(8,128)(2,1)S(1)} all-gather(bf16[32,256]{1,0:T(8,128)(2,1)} %param.21), channel_id=1, replica_groups=mesh['dp'=16,'seq'=2] {'dp','seq'}, dimensions={0}, use_global_device_ids=true | all-gather | bytes 540672 | tf_op jit(solution)/shard_map/all_gather | solution.py:152
  109.4 10.5 fusion.12
  131.5 10.3 fusion.8
  143.8 8.0 fusion.23
  151.8 38.7 %all_gather.77 = bf16[1024,256]{1,0:T(8,128)(2,1)S(1)} all-gather(bf16[32,256]{1,0:T(8,128)(2,1)S(1)} %copy-done.125), channel_id=1, replica_groups=mesh['dp'=16,'seq'=2] {'dp','seq'}, dimensions={0}, use_global_device_ids=true | all-gather | bytes 540672 | tf_op jit(solution)/shard_map/all_gather | solution.py:151
  194.3 12.0 all-gather.1
  222.4 12.9 fusion
  241.6 9.4 fusion.174
  251.0 14.6 while.44
  265.7 8.2 fusion.141
  274.0 11.7 fusion.177
  290.4 14.7 while.45
  305.1 8.2 fusion.139
  313.4 11.4 fusion.176
  327.8 9.4 fusion.178
  342.3 9.1 fusion.179
  351.4 60.0 %all-gather.26.cloned.1.call-done = bf16[2752,1024]{0,1:T(8,128)(2,1)} async-done(((bf16[2752,32]{0,1:T(8,128)(2,1)}), bf16[2752,1024]{0,1:T(8,128)(2,1)}) %all-gather.26.cloned.1.call-update) | async-done | bytes 5636112 | tf_op jit(solution)/shard_map/all_gather | solution.py:157
  411.4 13.9 multiply_convert_fusion.3
  425.3 6.7 fusion.183
  438.0 6.5 fusion.182
  450.9 12.9 multiply_convert_fusion.2
  482.2 9.3 fusion.137
  491.6 11.4 fusion.168
  503.1 9.8 multiply_convert_fusion.1
  512.9 11.8 bitcast_add_fusion.3
  524.8 8.6 slice_multiply_fusion.3
  533.3 7.8 multiply_reduce_fusion.7
  544.2 12.4 fusion.135
  559.8 9.9 bitcast_add_fusion.1
  573.6 11.0 fusion.169
  589.3 9.3 multiply_reduce_fusion.3
  598.8 8.8 multiply_convert_fusion
  614.4 14.5 while.46
  643.3 14.4 while.47
  693.8 8.7 fusion.128
  702.5 8.5 fusion.122
  711.1 7.8 fusion.71
  720.4 10.4 fusion.70
  765.1 6.5 convolution_add_fusion
  773.2 6.8 fusion.84
  796.8 40.2 %all-reduce.4 = (f32[1024]{0:T(1024)S(1)}, f32[1024]{0:T(1024)S(1)}) all-reduce(f32[1024]{0:T(1024)S(1)} %add.509, f32[1024]{0:T(1024)S(1)} %add.510), channel_id=17, replica_groups=mesh['dp'=16,'seq'=2] {'dp','seq'}, use_global_device_ids=true, to_apply=%region_39.40.clone | all-reduce | flops 2048 | bytes 16384
  843.8 38.4 %reduce-scatter.10.cloned.1.call-done = f32[32,256]{1,0:T(8,128)} async-done(((f32[1024,256]{1,0:T(8,128)}), f32[32,256]{1,0:T(8,128)}) %reduce-scatter.10.cloned.1.call-update) | async-done | bytes 32784 | tf_op jit(solution)/shard_map/reduce_scatter | solution.py:304
  882.2 139.7 %reduce-scatter.14.cloned.1.call-done = f32[32,1024]{1,0:T(8,128)} async-done(((f32[1024,1024]{1,0:T(8,128)}), f32[32,1024]{1,0:T(8,128)}) %reduce-scatter.14.cloned.1.call-update) | async-done | bytes 131088 | tf_op jit(solution)/shard_map/reduce_scatter | solution.py:306
  1021.9 140.0 %reduce-scatter.12.cloned.1.call-done = f32[32,1024]{1,0:T(8,128)} async-done(((f32[1024,1024]{1,0:T(8,128)}), f32[32,1024]{1,0:T(8,128)}) %reduce-scatter.12.cloned.1.call-update) | async-done | bytes 131088 | tf_op jit(solution)/shard_map/reduce_scatter | solution.py:305
  1161.8 153.6 %reduce-scatter.18.cloned.1.call-done = f32[32,2752]{1,0:T(8,128)} async-done(((f32[1024,2752]{1,0:T(8,128)}), f32[32,2752]{1,0:T(8,128)}) %reduce-scatter.18.cloned.1.call-update) | async-done | bytes 352272 | tf_op jit(solution)/shard_map/reduce_scatter | solution.py:308
  1315.4 153.4 %reduce-scatter.16.cloned.1.call-done = f32[32,2752]{1,0:T(8,128)} async-done(((f32[1024,2752]{1,0:T(8,128)}), f32[32,2752]{1,0:T(8,128)}) %reduce-scatter.16.cloned.1.call-update) | async-done | bytes 352272 | tf_op jit(solution)/shard_map/reduce_scatter | solution.py:307
  1468.8 153.5 %reduce-scatter.20.cloned.1.call-done = f32[2752,32]{0,1:T(8,128)} async-done(((f32[2752,1024]{0,1:T(8,128)}), f32[2752,32]{0,1:T(8,128)}) %reduce-scatter.20.cloned.1.call-update) | async-done | bytes 352272 | tf_op jit(solution)/shard_map/reduce_scatter | solution.py:309
  (467 shorter events, 291.3 us)
Async XLA Ops:
  7.2 96.1 %all-gather.18.cloned.1.call-start = ((), (), s32[]{:S(2)}) async-start(), calls=%async_computation.7 | async-start | bytes 2162688 | tf_op jit(solution)/shard_map/all_gather | solution.py:153
  7.9 243.1 %all-gather.28.cloned.1.call-start = ((), (), s32[]{:S(2)}) async-start(), calls=%async_computation.19 | async-start | bytes 4718592 | tf_op jit(solution)/shard_map/all_gather | solution.py:17
  51.7 140.1 %copy-start.103 = (f32[1024]{0:T(1024)}, f32[1024]{0:T(1024)S(1)}, u32[]{:S(2)}) copy-start(f32[1024]{0:T(1024)S(1)} %convert_element_type.274) | copy-start | bytes 12292
  51.7 92.1 %copy-start.114 = (f32[273]{0:T(512)}, f32[273]{0:T(512)S(1)}, u32[]{:S(2)}) copy-start(f32[273]{0:T(512)S(1)} %pad.13.clone) | copy-start | bytes 3280
  53.7 49.5 %copy-start.121 = (f32[512]{0:T(512)}, f32[512]{0:T(512)S(1)}, u32[]{:S(2)}) copy-start(f32[512]{0:T(512)S(1)} %get-tuple-element.851) | copy-start | bytes 6148
  53.7 67.3 %copy-start.123 = (f32[512]{0:T(512)}, f32[512]{0:T(512)S(1)}, u32[]{:S(2)}) copy-start(f32[512]{0:T(512)S(1)} %get-tuple-element.852) | copy-start | bytes 6148
  53.8 136.7 %copy-start.119 = (f32[512]{0:T(512)}, f32[512]{0:T(512)S(1)}, u32[]{:S(2)}) copy-start(f32[512]{0:T(512)S(1)} %fusion.145) | copy-start | bytes 6148
  95.8 25.3 %copy-start.48 = (bf16[1024,256]{1,0:T(8,128)(2,1)}, bf16[1024,256]{1,0:T(8,128)(2,1)S(1)}, u32[]{:S(2)}) copy-start(bf16[1024,256]{1,0:T(8,128)(2,1)S(1)} %all_gather.78) | copy-start | bytes 1572868
  98.5 45.3 %copy-start.55 = (f32[512,256]{0,1:T(8,128)}, f32[512,256]{0,1:T(8,128)S(1)}, u32[]{:S(2)}) copy-start(f32[512,256]{0,1:T(8,128)S(1)} %convert_multiply_fusion.3) | copy-start | bytes 1572868
  120.0 165.7 %all-gather.20.cloned.1.call-start = ((), (), s32[]{:S(2)}) async-start(), calls=%async_computation.8 | async-start | bytes 2162688 | tf_op jit(solution)/shard_map/all_gather | solution.py:154
  120.7 169.6 %all-gather.30.cloned.1.call-start = ((), (), s32[]{:S(2)}) async-start(), calls=%async_computation.20 | async-start | bytes 4718592 | tf_op jit(solution)/shard_map/all_gather | solution.py:17
  121.1 70.7 %copy-start.112 = (f32[512]{0:T(512)}, f32[512]{0:T(512)S(1)}, u32[]{:S(2)}) copy-start(f32[512]{0:T(512)S(1)} %fusion.147) | copy-start | bytes 6148
  121.7 98.2 %copy-start.67 = (bf16[512,256]{0,1:T(8,128)(2,1)}, bf16[512,256]{0,1:T(8,128)(2,1)S(1)}, u32[]{:S(2)}) copy-start(bf16[512,256]{0,1:T(8,128)(2,1)S(1)} %get-tuple-element.925) | copy-start | bytes 786436
  121.8 22.1 %copy-start.57 = (f32[512,256]{0,1:T(8,128)}, f32[512,256]{0,1:T(8,128)S(1)}, u32[]{:S(2)}) copy-start(f32[512,256]{0,1:T(8,128)S(1)} %convert_multiply_fusion.2) | copy-start | bytes 1572868
  141.8 186.0 %all-gather.22.cloned.1.call-start = ((), (), s32[]{:S(2)}) async-start(), calls=%async_computation.9 | async-start | bytes 5947392 | tf_op jit(solution)/shard_map/all_gather | solution.py:155
  142.4 199.9 %all-gather.24.cloned.1.call-start = ((), (), s32[]{:S(2)}) async-start(), calls=%async_computation.10 | async-start | bytes 5947392 | tf_op jit(solution)/shard_map/all_gather | solution.py:156
  143.0 268.4 %all-gather.26.cloned.1.call-start = ((), (), s32[]{:S(2)}) async-start(), calls=%async_computation.11 | async-start | bytes 5947392 | tf_op jit(solution)/shard_map/all_gather | solution.py:157
  143.8 470.6 %all-gather.32.cloned.1.call-start = ((), (), s32[]{:S(2)}) async-start(), calls=%async_computation.21 | async-start | bytes 4718592 | tf_op jit(solution)/shard_map/all_gather | solution.py:17
  191.8 19.3 %copy-start.40 = (f32[512,16,16]{0,2,1:T(8,128)}, f32[512,16,16]{0,2,1:T(8,128)S(1)}, u32[]{:S(2)}) copy-start(f32[512,16,16]{0,2,1:T(8,128)S(1)} %get-tuple-element.933) | copy-start | bytes 1572868
  193.1 21.3 %copy-start.38 = (f32[512,16,16]{0,2,1:T(8,128)}, f32[512,16,16]{0,2,1:T(8,128)S(1)}, u32[]{:S(2)}) copy-start(f32[512,16,16]{0,2,1:T(8,128)S(1)} %get-tuple-element.929) | copy-start | bytes 1572868
  222.3 12.9 copy-start.27
  222.4 12.9 copy-start.59
  235.2 38.7 %copy-start.109 = (f32[16,512]{1,0:T(8,128)}, f32[16,512]{1,0:T(8,128)S(1)}, u32[]{:S(2)}) copy-start(f32[16,512]{1,0:T(8,128)S(1)} %get-tuple-element.853) | copy-start | bytes 98308
  235.2 78.1 %copy-start.107 = (f32[16,512]{1,0:T(8,128)}, f32[16,512]{1,0:T(8,128)S(1)}, u32[]{:S(2)}) copy-start(f32[16,512]{1,0:T(8,128)S(1)} %get-tuple-element.854) | copy-start | bytes 98308
  251.0 14.6 copy-start.80
  251.0 14.6 copy-start.115
  290.4 14.7 copy-start.78
  327.8 14.6 copy-start.95
  425.3 19.2 %slice-start.8 = ((s8[5767168]{0:T(1024)(128)(4,1)}), s8[4194304]{0:T(1024)(128)(4,1)S(1)}, s32[]{:S(2)}) async-start(s8[5767168]{0:T(1024)(128)(4,1)} %bitcast.520), calls=%async_computation.31 | async-start | bytes 8388608
  432.5 12.0 slice-start.9
  470.1 12.1 slice-start.6
  503.0 140.3 %all-gather.34.cloned.1.call-start = ((), (), s32[]{:S(2)}) async-start(), calls=%async_computation.22 | async-start | bytes 4718592 | tf_op jit(solution)/shard_map/all_gather | solution.py:17
  512.9 43.7 %copy-start.6 = (bf16[16,512,512]{1,2,0:T(8,128)(2,1)}, bf16[16,512,512]{1,2,0:T(8,128)(2,1)S(1)}, u32[]{:S(2)}) copy-start(bf16[16,512,512]{1,2,0:T(8,128)(2,1)S(1)} %multiply_convert_fusion.1) | copy-start | bytes 25165828
  544.1 29.5 %copy-start.29 = (f32[512,1024]{0,1:T(8,128)}, f32[512,1024]{0,1:T(8,128)S(1)}, u32[]{:S(2)}) copy-start(f32[512,1024]{0,1:T(8,128)S(1)} %get-tuple-element.946) | copy-start | bytes 6291460
  544.1 12.5 copy-start.86
  544.1 29.5 %slice-start.4 = ((s8[8388608]{0:T(1024)(128)(4,1)}), s8[4194304]{0:T(1024)(128)(4,1)S(1)}, s32[]{:S(2)}) async-start(s8[8388608]{0:T(1024)(128)(4,1)} %bitcast.445), calls=%async_computation.27 | async-start | bytes 8388608
  556.6 17.0 %slice-start.5 = ((s8[8388608]{0:T(1024)(128)(4,1)}), s8[4194304]{0:T(1024)(128)(4,1)S(1)}, s32[]{:S(2)}) async-start(s8[8388608]{0:T(1024)(128)(4,1)} %bitcast.445), calls=%async_computation.28 | async-start | bytes 8388608
  598.7 245.2 %reduce-scatter.8.cloned.1.call-start = ((), (), s32[]{:S(2)}) async-start(), calls=%async_computation.12 | async-start | bytes 1081344 | tf_op jit(solution)/shard_map/reduce_scatter | solution.py:303
  614.3 267.9 %reduce-scatter.10.cloned.1.call-start = ((), (), s32[]{:S(2)}) async-start(), calls=%async_computation.13 | async-start | bytes 1081344 | tf_op jit(solution)/shard_map/reduce_scatter | solution.py:304
  666.1 14.3 slice-start.2
  686.3 335.6 %reduce-scatter.14.cloned.1.call-start = ((), (), s32[]{:S(2)}) async-start(), calls=%async_computation.15 | async-start | bytes 4325376 | tf_op jit(solution)/shard_map/reduce_scatter | solution.py:306
  692.6 469.2 %reduce-scatter.12.cloned.1.call-start = ((), (), s32[]{:S(2)}) async-start(), calls=%async_computation.14 | async-start | bytes 4325376 | tf_op jit(solution)/shard_map/reduce_scatter | solution.py:305
  693.8 17.2 %slice-start = ((s8[8388608]{0:T(1024)(128)(4,1)}), s8[4194304]{0:T(1024)(128)(4,1)S(1)}, s32[]{:S(2)}) async-start(s8[8388608]{0:T(1024)(128)(4,1)} %bitcast.432), calls=%async_computation.23 | async-start | bytes 8388608
  734.3 581.1 %reduce-scatter.18.cloned.1.call-start = ((), (), s32[]{:S(2)}) async-start(), calls=%async_computation.17 | async-start | bytes 11894784 | tf_op jit(solution)/shard_map/reduce_scatter | solution.py:308
  746.8 722.0 %reduce-scatter.16.cloned.1.call-start = ((), (), s32[]{:S(2)}) async-start(), calls=%async_computation.16 | async-start | bytes 11894784 | tf_op jit(solution)/shard_map/reduce_scatter | solution.py:307
  758.0 864.3 %reduce-scatter.20.cloned.1.call-start = ((), (), s32[]{:S(2)}) async-start(), calls=%async_computation.18 | async-start | bytes 11894784 | tf_op jit(solution)/shard_map/reduce_scatter | solution.py:309
  793.7 44.6 %copy-start.122 = (f32[512]{0:T(512)S(1)}, f32[512]{0:T(512)}, u32[]{:S(2)}) copy-start(f32[512]{0:T(512)} %copy-done.121) | copy-start | bytes 6148
  793.7 44.6 %copy-start.124 = (f32[512]{0:T(512)S(1)}, f32[512]{0:T(512)}, u32[]{:S(2)}) copy-start(f32[512]{0:T(512)} %copy-done.123) | copy-start | bytes 6148
  (112 other events, 576.2 us)
Sparse Core Ops, SparseCore 0:
  10.9 59.6 all-gather.17
  120.1 8.2 all-gather.27
  131.2 57.8 all-gather.19
  190.5 11.6 all-gather.29
  204.9 68.3 all-gather.21
  276.0 66.2 all-gather.23
  345.1 66.2 all-gather.25
  503.1 11.0 all-gather.31
  598.8 10.8 all-gather.33
  614.4 133.8 reduce-scatter.7
  751.3 130.8 reduce-scatter.9
  884.9 136.8 reduce-scatter.13
  1024.7 137.0 reduce-scatter.11
  1164.6 150.7 reduce-scatter.17
  1318.1 150.6 reduce-scatter.15
  1471.5 150.7 reduce-scatter.19
where the time goes:
time: 1640 us; the launch traced here: 1630 us
  waiting for transfers between devices  847 us (52%)
  matrix products  415 us (25%)
  blocking collectives  181 us (11%)
  other arithmetic  107 us (7%)
  local copies, waits for them, and re-layouts  61.4 us (4%)
    reduce_scatter x1, waiting for transfers between devices, per_device(): lax.psum_scatter(totals[5], ('dp', 'seq'), scatter_dimension=0, tiled=True)  154 us
    reduce_scatter x1, waiting for transfers between devices, per_device(): lax.psum_scatter(totals[6], ('dp', 'seq'), scatter_dimension=1, tiled=True)  154 us
    reduce_scatter x1, waiting for transfers between devices, per_device(): lax.psum_scatter(totals[4], ('dp', 'seq'), scatter_dimension=0, tiled=True)  153 us
    reduce_scatter x1, waiting for transfers between devices, per_device(): lax.psum_scatter(totals[2], ('dp', 'seq'), scatter_dimension=0, tiled=True)  140 us
    reduce_scatter x1, waiting for transfers between devices, per_device(): lax.psum_scatter(totals[3], ('dp', 'seq'), scatter_dimension=0, tiled=True)  140 us
    unnamed x2, blocking collectives  82.3 us
    all_gather x1, waiting for transfers between devices, per_device(): lax.all_gather(w_down, ('dp', 'seq'), axis=1, tiled=True)  60 us
    all_gather x1, blocking collectives, per_device(): lax.all_gather(w_key, ('dp', 'seq'), axis=0, tiled=True)  42 us
  transfers between devices with their start and end apart: 16, of which 8 were waited for; matrix products, arithmetic and copies ran while one was open for 28% of the time, Pallas kernels for 0%

commit v1 on v0

v1 whole, which is shorter than its diff:
```python
import functools

import jax
import jax.numpy as jnp
import numpy as np
from jax import lax
from jax.experimental import pallas as pl
from jax.experimental.pallas import tpu as pltpu
from jax.sharding import PartitionSpec as P

H = 16
F = 16
DV = 64
AXES = ("dp", "seq")
EPS = 1e-06
TB = 256
TILE = 256
F32 = jnp.float32
BF16 = jnp.bfloat16

NN = (((1,), (0,)), ((), ()))
NT = (((1,), (1,)), ((), ()))
TN = (((0,), (0,)), ((), ()))


def dot(a, b, dims=NN):
    return lax.dot_general(a, b, dims, preferred_element_type=F32)


VMEM = pl.BlockSpec(memory_space=pltpu.VMEM)
SMEM = pl.BlockSpec(memory_space=pltpu.SMEM)


def params(mib, **kw):
    return pltpu.CompilerParams(vmem_limit_bytes=mib << 20, **kw)


def cost(flops, nbytes, trans=0):
    return pl.CostEstimate(flops=int(flops), bytes_accessed=int(nbytes), transcendentals=int(trans))


def sds(shape, dtype):
    return jax.ShapeDtypeStruct(shape, dtype)


def stage_orders(bits):
    straight = list(range(bits))
    swapped = [1, 0] + list(range(2, bits)) if bits > 1 else straight
    return (straight, swapped)


def stage_pairs(dp, bits, stage):
    orders = stage_orders(bits)
    return [
        (d * 2 + c, (d ^ (1 << orders[c][stage])) * 2 + c) for d in range(dp) for c in range(2)
    ]


def core_pairs(dp):
    return [(i, i ^ 1) for i in range(2 * dp)]


def block_tables(dp, bits):
    orders = stage_orders(bits)
    count = 2 * dp
    position = np.arange(count)
    masks = []
    for c in range(2):
        mask = np.zeros(count, np.int32)
        for stage in range(bits):
            mask |= ((position >> (bits - 1 - stage)) & 1) << orders[c][stage]
        masks.append(mask)
    d = lax.axis_index("dp").astype(jnp.int32)
    c = lax.axis_index("seq").astype(jnp.int32)
    owner_core = jnp.asarray(position >> bits, jnp.int32) ^ c
    mask = jnp.where(owner_core == 0, jnp.asarray(masks[0]), jnp.asarray(masks[1]))
    block_at = (d ^ mask) * 2 + owner_core
    block_core = jnp.asarray(position & 1, jnp.int32)
    apart = jnp.asarray(position >> 1, jnp.int32) ^ d
    places = []
    for k in range(2):
        place = jnp.zeros(count, jnp.int32)
        for stage in range(bits):
            place = place | (((apart >> orders[k][stage]) & 1) << (bits - 1 - stage))
        places.append(place)
    place_of = jnp.where(block_core == 0, places[0], places[1]) | ((block_core ^ c) << bits)
    return jnp.concatenate([block_at, place_of, c[None], jnp.zeros(7, jnp.int32)]), c


def gather(shard, dp, bits):
    held = shard
    for stage in reversed(range(bits)):
        came = lax.ppermute(held, AXES, stage_pairs(dp, bits, stage))
        if stage > 0:
            held = jnp.concatenate([held, came], axis=-2)
    swap = core_pairs(dp)
    return (held, came, lax.ppermute(held, AXES, swap), lax.ppermute(came, AXES, swap))


def reduce_rows(keep, send, dp, bits):
    came = lax.ppermute(send, AXES, core_pairs(dp))
    for stage in range(bits):
        half = keep.shape[-2] // 2
        send = (
            lax.slice_in_dim(keep, half, 2 * half, axis=keep.ndim - 2).astype(F32)
            + lax.slice_in_dim(came, half, 2 * half, axis=keep.ndim - 2).astype(F32)
        ).astype(BF16)
        keep = (
            lax.slice_in_dim(keep, 0, half, axis=keep.ndim - 2).astype(F32)
            + lax.slice_in_dim(came, 0, half, axis=keep.ndim - 2).astype(F32)
        ).astype(BF16)
        came = lax.ppermute(send, AXES, stage_pairs(dp, bits, stage))
    return keep.astype(F32) + came.astype(F32)


def pre_kernel(rows, count, tab, x, xr, y, yr, xt, r1, yt, yn, buf):
    c = tab[2 * count]
    half, width = xr.shape
    total = jnp.zeros((1, 2 * half), F32)
    for src, rec, dst in ((x, xr, xt), (y, yr, yt)):
        for i in range(half // 128):
            own = pl.multiple_of(c * half + i * 128, 128)
            other = pl.multiple_of((1 - c) * half + i * 128, 128)
            buf[:, pl.ds(own, 128)] = src[c, i * 128 : (i + 1) * 128, :].T.astype(buf.dtype)
            buf[:, pl.ds(other, 128)] = rec[i * 128 : (i + 1) * 128, :].T.astype(buf.dtype)

        def move(p, _):
            at = pl.multiple_of(tab[p] * rows, rows)
            dst[pl.ds(pl.multiple_of(p * rows, rows), rows), :] = buf[pl.ds(at, rows), :]
            return 0

        lax.fori_loop(0, count, move, 0)
    for i in range(width // 128):
        part = xt[i * 128 : (i + 1) * 128, :].astype(F32)
        total = total + jnp.sum(part * part, axis=0, keepdims=True)
        yn[:, i * 128 : (i + 1) * 128] = yt[i * 128 : (i + 1) * 128, :].T.astype(BF16)
    r1[...] = lax.rsqrt(total / width + EPS)


def pre(tab, x, xr, y, yr, rows, count, kind):
    half, width = xr.shape
    tokens = 2 * half
    return pl.pallas_call(
        functools.partial(pre_kernel, rows, count),
        out_shape=(
            sds((width, tokens), kind),
            sds((1, tokens), F32),
            sds((width, tokens), kind),
            sds((tokens, width), BF16),
        ),
        in_specs=[SMEM] + [VMEM] * 4,
        out_specs=[VMEM] * 4,
        scratch_shapes=[pltpu.VMEM((width, tokens), kind)],
        compiler_params=params(40),
        cost_estimate=cost(8 * width * tokens, 14 * width * tokens),
        name="pre",
    )(tab, x, xr, y, yr)


def project_kernel(xt, r1, w0, w1, w2, w3, normed, out):
    scale = r1[...]
    wide = out.shape[0]
    quarter = w0.shape[0]
    for q, w in enumerate((w0, w1, w2, w3)):
        gain = w[:, wide : wide + 1].astype(F32)
        part = xt[q * quarter : (q + 1) * quarter, :].astype(F32)
        normed[q * quarter : (q + 1) * quarter, :] = (part * scale * gain).astype(BF16)

    def tile(i, _):
        at = pl.multiple_of(i * 256, 256)
        acc = dot(w0[:, pl.ds(at, 256)], normed[0:quarter, :], TN)
        for q, w in ((1, w1), (2, w2), (3, w3)):
            acc = acc + dot(
                w[:, pl.ds(at, 256)], normed[q * quarter : (q + 1) * quarter, :], TN
            )
        out[pl.ds(at, 256), :] = acc.astype(BF16)
        return 0

    lax.fori_loop(0, wide // 256, tile, 0)


def project(xt, r1, bufs, wide):
    width, tokens = xt.shape
    return pl.pallas_call(
        project_kernel,
        out_shape=(sds((width, tokens), BF16), sds((wide, tokens), BF16)),
        in_specs=[VMEM] * 6,
        out_specs=[VMEM] * 2,
        compiler_params=params(40),
        cost_estimate=cost(2 * width * tokens * wide, 2 * (2 * width * tokens + 2 * wide * tokens)),
        name="project",
    )(xt, r1, *bufs)


def unit_rows(tokens, ones):
    row = lax.broadcasted_iota(jnp.int32, (16, tokens), 0)
    return jnp.where(row < ones, 1.0, 0.0).astype(BF16)


def causal(shape):
    j = lax.broadcasted_iota(jnp.int32, shape, 0)
    t = lax.broadcasted_iota(jnp.int32, shape, 1)
    return j <= t


def attend_kernel(rows, count, tab, q, k, v, att, den):
    h = pl.program_id(0)
    tokens = q.shape[1]
    one = unit_rows(tokens, 1)
    qa = jnp.concatenate([q[...] * jnp.asarray(F ** -0.5, BF16), one], axis=0)
    ka = jnp.concatenate([k[...], one], axis=0)
    va = jnp.concatenate([v[...], one], axis=0)
    below = causal((TB, TB))
    for b in range(tokens // TB):
        lo, hi = b * TB, (b + 1) * TB
        u = dot(ka[:, :hi], qa[:, lo:hi], TN)
        p = u * u + 1.0
        last = jnp.where(below, p[lo:], 0.0).astype(BF16)
        p = jnp.concatenate([p[:lo].astype(BF16), last], axis=0) if b else last
        o = dot(va[:, :hi], p)
        d = o[DV : DV + 1]
        done = o[:DV] / d
        den[0, :, lo:hi] = d
        for i in range(DV // rows):
            at = tab[count + h * (DV // rows) + i]
            att[pl.ds(pl.multiple_of(at * rows, rows), rows), lo:hi] = done[
                i * rows : (i + 1) * rows
            ].astype(att.dtype)


def head_specs(tokens):
    return [
        pl.BlockSpec((F, tokens), lambda h: (h, 0)),
        pl.BlockSpec((F, tokens), lambda h: (H + h, 0)),
        pl.BlockSpec((DV, tokens), lambda h: (2 * H * F // DV + h, 0)),
    ]


def attend(tab, qkv, rows, count, kind):
    tokens = qkv.shape[1]
    return pl.pallas_call(
        functools.partial(attend_kernel, rows, count),
        grid=(H,),
        out_shape=(sds((H * DV, tokens), kind), sds((H, 1, tokens), F32)),
        in_specs=[SMEM] + head_specs(tokens),
        out_specs=[
            pl.BlockSpec((H * DV, tokens), lambda h: (0, 0)),
            pl.BlockSpec((1, 1, tokens), lambda h: (h, 0, 0)),
        ],
        compiler_params=params(40),
        cost_estimate=cost(H * tokens * tokens * 256 * 2, 4 * H * DV * tokens * 2),
        name="attend",
    )(tab, qkv, qkv, qkv)


def middle_kernel(rows, count, tab, att, w0, w1, w2, w3, xt, gains, res, r2, x2t, x2, buf):
    width, tokens = xt.shape
    quarter = w0.shape[0]

    def tile(i, _):
        at = pl.multiple_of(i * 256, 256)
        acc = dot(w0[:, pl.ds(at, 256)], att[0:quarter, :], TN)
        for q, w in ((1, w1), (2, w2), (3, w3)):
            acc = acc + dot(w[:, pl.ds(at, 256)], att[q * quarter : (q + 1) * quarter, :], TN)
        buf[pl.ds(at, 256), :] = acc
        return 0

    lax.fori_loop(0, width // 256, tile, 0)

    def join(p, total):
        here = pl.ds(pl.multiple_of(p * rows, rows), rows)
        part = buf[pl.ds(pl.multiple_of(tab[p] * rows, rows), rows), :] + xt[here, :].astype(F32)
        res[here, :] = part
        return total + jnp.sum(part * part, axis=0, keepdims=True)

    total = lax.fori_loop(0, count, join, jnp.zeros((1, tokens), F32))
    scale = lax.rsqrt(total / width + EPS)
    r2[...] = scale

    def finish(i, _):
        at = pl.multiple_of(i * 128, 128)
        part = res[pl.ds(at, 128), :]
        low = (part * scale * gains[pl.ds(at, 128), 1:2].astype(F32)).astype(BF16)
        x2t[pl.ds(at, 128), :] = low
        x2[:, pl.ds(at, 128)] = low.T
        return 0

    lax.fori_loop(0, width // 128, finish, 0)


def middle(tab, att, bufs, xt, gains, rows, count):
    width, tokens = xt.shape
    return pl.pallas_call(
        functools.partial(middle_kernel, rows, count),
        out_shape=(
            sds((width, tokens), F32),
            sds((1, tokens), F32),
            sds((width, tokens), BF16),
            sds((tokens, width), BF16),
        ),
        in_specs=[SMEM] + [VMEM] * 7,
        out_specs=[VMEM] * 4,
        scratch_shapes=[pltpu.VMEM((width, tokens), F32)],
        compiler_params=params(48),
        cost_estimate=cost(2 * width * tokens * H * DV, 16 * width * tokens),
        name="middle",
    )(tab, att, *bufs, xt, gains)


def forward_kernel(x2, x2t, dy, dyt, w0, w1, w2, w3, hid, dgate, dup, send, keep):
    quarter = w0.shape[1]
    bufs = (w0, w1, w2, w3)

    def over(a, which):
        acc = dot(a[:, 0:quarter], w0[which])
        for q in range(1, 4):
            acc = acc + dot(a[:, q * quarter : (q + 1) * quarter], bufs[q][which])
        return acc

    gate = over(x2, 0)
    up = over(x2, 1)
    back = over(dy, 2)
    sig = 1.0 / (1.0 + jnp.exp(-gate))
    act = gate * sig
    h = (act * up).astype(BF16)
    dg = (back * up * sig * (1.0 + gate * (1.0 - sig))).astype(BF16)
    du = (back * act).astype(BF16)
    hid[...] = h
    dgate[...] = dg
    dup[...] = du
    half = keep.shape[1]
    for i, (a, b) in enumerate(((x2t, dg), (x2t, du), (dyt, h))):
        keep[i] = dot(a[:half, :], b).astype(BF16)
        send[i] = dot(a[half:, :], b).astype(BF16)


def forward_group(x2, x2t, dy, dyt, bufs):
    tokens, width = x2.shape
    cols = bufs[0].shape[-1]
    quarter = bufs[0].shape[1]
    col = pl.BlockSpec((tokens, TILE), lambda i: (0, i))
    return pl.pallas_call(
        forward_kernel,
        grid=(cols // TILE,),
        out_shape=(sds((tokens, cols), BF16),) * 3 + (sds((3, width // 2, cols), BF16),) * 2,
        in_specs=[VMEM] * 4 + [pl.BlockSpec((3, quarter, TILE), lambda i: (0, 0, i))] * 4,
        out_specs=[col] * 3 + [pl.BlockSpec((3, width // 2, TILE), lambda i: (0, 0, i))] * 2,
        compiler_params=params(40),
        cost_estimate=cost(12 * tokens * width * cols, 2 * (4 * tokens * width + 9 * width * cols)),
        name="forward_group",
    )(x2, x2t, dy, dyt, *bufs)


def group_layout(groups):
    tiles = [g // TILE for g in groups]
    starts = [sum(tiles[:i]) for i in range(len(tiles))]
    return tiles, starts


def pulled(groups, which, left_refs, weight_refs, acc):
    tiles, starts = group_layout(groups)
    step = pl.program_id(0)

    @pl.when(step == 0)
    def _():
        acc[...] = jnp.zeros_like(acc)

    for g in range(len(groups)):

        @pl.when((step >= starts[g]) & (step < starts[g] + tiles[g]))
        def _(g=g):
            for b in range(4):
                w = weight_refs[g * 4 + b]
                quarter = w.shape[1]
                part = acc[:, b * quarter : (b + 1) * quarter]
                for k in range(len(which)):
                    part = part + dot(left_refs[g * len(which) + k][...], w[k], NT)
                acc[:, b * quarter : (b + 1) * quarter] = part


def pull_specs(groups, first, many, tokens, quarter):
    tiles, starts = group_layout(groups)
    left, weights = [], []
    for g in range(len(groups)):
        col = functools.partial(
            lambda i, s, n: jnp.clip(i - s, 0, n - 1), s=starts[g], n=tiles[g]
        )
        left += [pl.BlockSpec((tokens, TILE), lambda i, col=col: (0, col(i)))] * many
        weights += [
            pl.BlockSpec(
                (many, quarter, TILE), lambda i, col=col: (first // many, 0, col(i))
            )
        ] * 4
    return left, weights


def back_kernel(groups, rows, count, tab, *refs):
    G = len(groups)
    lefts, weights = refs[: 2 * G], refs[2 * G : 6 * G]
    res, r2, yt, gains, dres, dm, acc, dmf = refs[6 * G :]
    pulled(groups, (0, 1), lefts, weights, acc)

    @pl.when(pl.program_id(0) == pl.num_programs(0) - 1)
    def _():
        tokens, width = acc.shape
        scale = r2[...]

        def first(i, total):
            at = pl.multiple_of(i * 128, 128)
            part = acc[:, pl.ds(at, 128)].T * gains[pl.ds(at, 128), 1:2].astype(F32)
            dres[pl.ds(at, 128), :] = part
            return total + jnp.sum(part * res[pl.ds(at, 128), :], axis=0, keepdims=True)

        total = lax.fori_loop(0, width // 128, first, jnp.zeros((1, tokens), F32))
        pull = total / width * scale * scale * scale

        def second(p, _):
            here = pl.ds(pl.multiple_of(p * rows, rows), rows)
            part = yt[here, :].astype(F32) + scale * dres[here, :] - res[here, :] * pull
            dres[here, :] = part
            dmf[pl.ds(pl.multiple_of(tab[p] * rows, rows), rows), :] = part.astype(dmf.dtype)
            return 0

        lax.fori_loop(0, count, second, 0)
        dm[...] = dmf[...].astype(BF16)


def back(tab, dgates, dups, bufs, res, r2, yt, gains, groups, rows, count, kind):
    width, tokens = res.shape
    quarter = width // 4
    cols = sum(groups)
    lefts = [a for pair in zip(dgates, dups) for a in pair]
    weights = [b for four in bufs for b in four]
    left, weight = pull_specs(groups, 0, 2, tokens, quarter)
    return pl.pallas_call(
        functools.partial(back_kernel, groups, rows, count),
        grid=(cols // TILE,),
        out_shape=(sds((width, tokens), F32), sds((width, tokens), BF16)),
        in_specs=[SMEM] + left + weight + [VMEM] * 4,
        out_specs=[VMEM] * 2,
        scratch_shapes=[pltpu.VMEM((tokens, width), F32), pltpu.VMEM((width, tokens), kind)],
        compiler_params=params(52),
        cost_estimate=cost(4 * tokens * width * cols, 8 * width * cols + 16 * width * tokens),
        name="back",
    )(tab, *lefts, *weights, res, r2, yt, gains)


def output_kernel(groups, rows, count, tab, *refs):
    G = len(groups)
    lefts, weights = refs[:G], refs[G : 5 * G]
    res, out, acc, nat = refs[5 * G :]
    pulled(groups, (2,), lefts, weights, acc)

    @pl.when(pl.program_id(0) == pl.num_programs(0) - 1)
    def _():
        tokens, width = acc.shape

        def first(i, _):
            at = pl.multiple_of(i * 128, 128)
            part = acc[:, pl.ds(at, 128)].T + res[pl.ds(at, 128), :]
            for k in range(128 // rows):
                to = tab[i * (128 // rows) + k]
                nat[pl.ds(pl.multiple_of(to * rows, rows), rows), :] = part[
                    k * rows : (k + 1) * rows
                ].astype(nat.dtype)
            return 0

        lax.fori_loop(0, width // 128, first, 0)

        def second(i, _):
            at = pl.multiple_of(i * 128, 128)
            out[:, pl.ds(at, 128)] = nat[pl.ds(at, 128), :].T.astype(BF16)
            return 0

        lax.fori_loop(0, width // 128, second, 0)


def output_of(tab, hids, bufs, res, groups, rows, count, kind):
    width, tokens = res.shape
    quarter = width // 4
    cols = sum(groups)
    weights = [b for four in bufs for b in four]
    left, weight = pull_specs(groups, 2, 1, tokens, quarter)
    return pl.pallas_call(
        functools.partial(output_kernel, groups, rows, count),
        grid=(cols // TILE,),
        out_shape=sds((tokens, width), BF16),
        in_specs=[SMEM] + left + weight + [VMEM],
        out_specs=VMEM,
        scratch_shapes=[pltpu.VMEM((tokens, width), F32), pltpu.VMEM((width, tokens), kind)],
        compiler_params=params(40),
        cost_estimate=cost(2 * tokens * width * cols, 4 * width * cols + 6 * width * tokens),
        name="output_of",
    )(tab, *hids, *weights, res)


def mixed_kernel(dm, att, w0, w1, w2, w3, send, keep, datt):
    quarter = w0.shape[0]
    half = keep.shape[0]
    for q, w in enumerate((w0, w1, w2, w3)):
        datt[q * quarter : (q + 1) * quarter, :] = dot(w[...], dm[...])

    def tile(i, _):
        at = pl.multiple_of(i * 256, 256)
        right = dm[pl.ds(at, 256), :]
        keep[:, pl.ds(at, 256)] = dot(att[:half, :], right, NT).astype(BF16)
        send[:, pl.ds(at, 256)] = dot(att[half:, :], right, NT).astype(BF16)
        return 0

    lax.fori_loop(0, dm.shape[0] // 256, tile, 0)


def mixed(dm, att, bufs):
    width, tokens = dm.shape
    rows = att.shape[0]
    return pl.pallas_call(
        mixed_kernel,
        out_shape=(sds((rows // 2, width), BF16),) * 2 + (sds((rows, tokens), F32),),
        in_specs=[VMEM] * 6,
        out_specs=[VMEM] * 3,
        compiler_params=params(40),
        cost_estimate=cost(4 * width * tokens * rows, 12 * width * tokens),
        name="mixed",
    )(dm, att, *bufs)


def attend_back_kernel(rows, count, tab, q, k, v, datt, att, den, dq, dk, dv, acc):
    h = pl.program_id(0)
    tokens = q.shape[1]
    scale = jnp.asarray(F ** -0.5, BF16)
    da, done = [], []
    for i in range(DV // rows):
        at = pl.multiple_of(tab[count + h * (DV // rows) + i] * rows, rows)
        da.append(datt[pl.ds(at, rows), :])
        done.append(att[pl.ds(at, rows), :].astype(F32))
    da = jnp.concatenate(da, axis=0) if len(da) > 1 else da[0]
    done = jnp.concatenate(done, axis=0) if len(done) > 1 else done[0]
    inv = 2.0 / den[0]
    dn = (da * inv).astype(BF16)
    dd = -jnp.sum(da * done, axis=0, keepdims=True) * inv
    dd_high = dd.astype(BF16).astype(F32)
    row = lax.broadcasted_iota(jnp.int32, (16, tokens), 0)
    tail = jnp.where(row == 0, dd_high, jnp.where(row == 1, dd - dd_high, 0.0)).astype(BF16)
    one = unit_rows(tokens, 1)
    qs = q[...] * scale
    ks = k[...] * scale
    qa = jnp.concatenate([qs, one], axis=0)
    ka = jnp.concatenate([k[...], one], axis=0)
    va = jnp.concatenate([v[...], unit_rows(tokens, 2)], axis=0)
    na = jnp.concatenate([dn, tail], axis=0)
    zero = jnp.zeros((DV, tokens), BF16)
    right_p = jnp.concatenate([dn * jnp.asarray(0.5, BF16), zero], axis=0).T
    right_s = jnp.concatenate([zero, qs, jnp.zeros((DV - F, tokens), BF16)], axis=0).T
    below = causal((TB, TB))
    for b in range(tokens // TB):
        lo, hi = b * TB, (b + 1) * TB
        u = dot(ka[:, :hi], qa[:, lo:hi], TN)
        g = dot(va[:, :hi], na[:, lo:hi], TN)
        p = u * u + 1.0
        s = g * u
        p_last = jnp.where(below, p[lo:], 0.0).astype(BF16)
        s_last = jnp.where(below, s[lo:], 0.0).astype(BF16)
        if b:
            p = jnp.concatenate([p[:lo].astype(BF16), p_last], axis=0)
            s = jnp.concatenate([s[:lo].astype(BF16), s_last], axis=0)
        else:
            p, s = p_last, s_last
        dq[:, lo:hi] = dot(ks[:, :hi], s).astype(BF16)
        both = dot(p, right_p[lo:hi]) + dot(s, right_s[lo:hi])
        if b:
            acc[:lo, :] = acc[:lo, :] + both[:lo]
        acc[lo:hi, :] = both[lo:]
    turned = acc[...].T
    dv[...] = turned[:DV].astype(BF16)
    dk[...] = turned[DV : DV + F].astype(BF16)


def attend_back(tab, qkv, datt, att, den, rows, count):
    tokens = qkv.shape[1]
    return pl.pallas_call(
        functools.partial(attend_back_kernel, rows, count),
        grid=(H,),
        out_shape=(
            sds((H * F, tokens), BF16),
            sds((H * F, tokens), BF16),
            sds((H * DV, tokens), BF16),
        ),
        in_specs=[SMEM]
        + head_specs(tokens)
        + [VMEM, VMEM, pl.BlockSpec((1, 1, tokens), lambda h: (h, 0, 0))],
        out_specs=[
            pl.BlockSpec((F, tokens), lambda h: (h, 0)),
            pl.BlockSpec((F, tokens), lambda h: (h, 0)),
            pl.BlockSpec((DV, tokens), lambda h: (h, 0)),
        ],
        scratch_shapes=[pltpu.VMEM((tokens, 2 * DV), F32)],
        compiler_params=params(40),
        cost_estimate=cost(H * tokens * tokens * 256 * 6, 8 * H * DV * tokens * 2),
        name="attend_back",
    )(tab, qkv, qkv, qkv, datt, att, den)


def weights_kernel(normed, dq, dk, dv, send, keep):
    half = keep.shape[0]
    at = 0
    for ref in (dq, dk, dv):
        for i in range(ref.shape[0] // 256):
            right = ref[i * 256 : (i + 1) * 256, :]
            keep[:, at : at + 256] = dot(normed[:half, :], right, NT).astype(BF16)
            send[:, at : at + 256] = dot(normed[half:, :], right, NT).astype(BF16)
            at += 256


def weights_of(normed, dq, dk, dv):
    width, tokens = normed.shape
    wide = dq.shape[0] + dk.shape[0] + dv.shape[0]
    return pl.pallas_call(
        weights_kernel,
        out_shape=(sds((width // 2, wide), BF16),) * 2,
        in_specs=[VMEM] * 4,
        out_specs=[VMEM] * 2,
        compiler_params=params(32),
        cost_estimate=cost(2 * width * tokens * wide, 6 * width * tokens + 4 * width * wide),
        name="weights_of",
    )(normed, dq, dk, dv)


def input_kernel(rows, count, tab, dq, dk, dv, w0, w1, w2, w3, gains, dres, xt, r1, out, buf, nat):
    width, tokens = xt.shape
    quarter = w0.shape[0]
    a, b, c = dq.shape[0], dk.shape[0], dv.shape[0]
    total = jnp.zeros((1, tokens), F32)
    scale = r1[...]
    for q, w in enumerate((w0, w1, w2, w3)):
        here = slice(q * quarter, (q + 1) * quarter)
        part = dot(w[:, :a], dq[...]) + dot(w[:, a : a + b], dk[...])
        part = part + dot(w[:, a + b : a + b + c], dv[...])
        part = part * gains[here, 0:1].astype(F32)
        buf[here, :] = part
        total = total + jnp.sum(part * xt[here, :].astype(F32), axis=0, keepdims=True)
    pull = total / width * scale * scale * scale

    def second(p, _):
        here = pl.ds(pl.multiple_of(p * rows, rows), rows)
        part = dres[here, :] + scale * buf[here, :] - xt[here, :].astype(F32) * pull
        nat[pl.ds(pl.multiple_of(tab[p] * rows, rows), rows), :] = part.astype(nat.dtype)
        return 0

    lax.fori_loop(0, count, second, 0)

    def third(i, _):
        at = pl.multiple_of(i * 128, 128)
        out[:, pl.ds(at, 128)] = nat[pl.ds(at, 128), :].T.astype(BF16)
        return 0

    lax.fori_loop(0, width // 128, third, 0)


def input_of(tab, dq, dk, dv, bufs, gains, dres, xt, r1, rows, count, kind):
    width, tokens = xt.shape
    wide = dq.shape[0] + dk.shape[0] + dv.shape[0]
    return pl.pallas_call(
        functools.partial(input_kernel, rows, count),
        out_shape=sds((tokens, width), BF16),
        in_specs=[SMEM] + [VMEM] * 11,
        out_specs=VMEM,
        scratch_shapes=[pltpu.VMEM((width, tokens), F32), pltpu.VMEM((width, tokens), kind)],
        compiler_params=params(48),
        cost_estimate=cost(2 * width * tokens * wide, 12 * width * tokens + 2 * wide * tokens),
        name="input_of",
    )(tab, dq, dk, dv, *bufs, gains, dres, xt, r1)


def split_columns(total):
    tiles = -(-total // TILE)
    first = -(-tiles // 3)
    second = -(-(tiles - first) // 2)
    return [n * TILE for n in (first, second, tiles - first - second)]


def per_device(
    inputs, w_query, w_key, w_value, w_out, w_gate, w_up, w_down, gain_one, gain_two, cotangent
):
    dp = lax.axis_size("dp")
    bits = dp.bit_length() - 1
    count = 2 * dp
    micro, _, half, width = inputs.shape
    rows = width // count
    kind = BF16 if rows % 16 == 0 else F32
    hidden = w_gate.shape[1]
    groups = split_columns(hidden)
    padded = sum(groups)
    tab, core = block_tables(dp, bits)
    swap = core_pairs(dp)

    x = inputs.reshape(micro, half, width)
    y = cotangent.reshape(micro, half, width)
    x_sent = lax.dynamic_index_in_dim(x, 1 - core, 0, keepdims=False)
    y_sent = lax.dynamic_index_in_dim(y, 1 - core, 0, keepdims=False)
    x_came = lax.ppermute(x_sent, AXES, swap)
    y_came = lax.ppermute(y_sent, AXES, swap)

    wide = w_query.shape[1] + w_key.shape[1] + w_value.shape[1]
    pair = jnp.pad(jnp.stack([gain_one, gain_two], axis=1), ((0, 0), (0, 126)))
    own_qkv = jnp.concatenate([w_query, w_key, w_value], axis=1)
    qkv_bufs = gather(jnp.concatenate([own_qkv, pair], axis=1), dp, bits)
    out_bufs = gather(w_out, dp, bits)
    fill = ((0, 0), (0, padded - hidden))
    ff_own = jnp.stack([jnp.pad(w_gate, fill), jnp.pad(w_up, fill), jnp.pad(w_down.T, fill)])
    ff_bufs, at = [], 0
    for n in groups:
        ff_bufs.append(gather(ff_own[:, :, at : at + n], dp, bits))
        at += n

    xt, r1, yt, yn = pre(tab, x, x_came, y, y_came, rows, count, kind)
    xt, yt_low = xt.astype(BF16), yt.astype(BF16)
    gains = jnp.concatenate([b[:, wide:] for b in qkv_bufs], axis=0)
    normed, qkv = project(xt, r1, qkv_bufs, wide)
    att_any, den = attend(tab, qkv, rows, count, kind)
    att = att_any.astype(BF16)
    res, r2, x2t, x2 = middle(tab, att, out_bufs, xt, gains, rows, count)
    hids, dgates, dups, ff_grads = [], [], [], []
    for bufs in ff_bufs:
        hid, dgate, dup, send, keep = forward_group(x2, x2t, yn, yt_low, bufs)
        hids.append(hid)
        dgates.append(dgate)
        dups.append(dup)
        ff_grads.append(reduce_rows(keep, send, dp, bits))
    dres, dm = back(tab, dgates, dups, ff_bufs, res, r2, yt_low, gains, groups, rows, count, kind)
    send, keep, datt = mixed(dm, att, out_bufs)
    grad_out = reduce_rows(keep, send, dp, bits)
    dq, dk, dv = attend_back(tab, qkv, datt, att_any, den, rows, count)
    send, keep = weights_of(normed, dq, dk, dv)
    grad_qkv = reduce_rows(keep, send, dp, bits)
    output = output_of(tab, hids, ff_bufs, res, groups, rows, count, kind)
    dx = input_of(tab, dq, dk, dv, qkv_bufs, gains, dres, xt, r1, rows, count, kind)

    def give_back(value):
        mine = lax.dynamic_slice_in_dim(value, core * half, half, 0)
        other = lax.dynamic_slice_in_dim(value, (1 - core) * half, half, 0)
        came = lax.ppermute(other, AXES, swap)
        both = jnp.where(core == 0, jnp.stack([mine, came]), jnp.stack([came, mine]))
        return both.reshape(micro, 1, half, width)

    ff = jnp.concatenate(ff_grads, axis=-1)[:, :, :hidden]
    a, b = w_query.shape[1], w_query.shape[1] + w_key.shape[1]
    gain_one_grad = jnp.sum(own_qkv.astype(F32) * grad_qkv, axis=1) / gain_one.astype(F32)
    gain_two_grad = (
        jnp.sum(w_gate.astype(F32) * ff[0] + w_up.astype(F32) * ff[1], axis=1)
    ) / gain_two.astype(F32)
    return (
        give_back(output),
        give_back(dx),
        grad_qkv[:, :a],
        grad_qkv[:, a:b],
        grad_qkv[:, b:],
        grad_out,
        ff[0],
        ff[1],
        ff[2].T,
        gain_one_grad,
        gain_two_grad,
    )


def solution(mesh):
    shard = P(AXES, None)
    batch = P(None, "dp", "seq", None)
    return jax.shard_map(
        per_device,
        mesh=mesh,
        in_specs=(batch,) + (shard,) * 6 + (P(None, AXES), P(AXES), P(AXES), batch),
        out_specs=(batch,) * 2 + (shard,) * 6 + (P(None, AXES), P(AXES), P(AXES)),
        check_vma=False,
    )
```

time: 1640 us -> 527 us (0.32)
  waiting for transfers between devices: 847 us -> 161 us
  matrix products: 415 us -> 0 us
  Pallas kernels: 0 us -> 216 us
  blocking collectives: 181 us -> 0 us
  other arithmetic: 107 us -> 26.1 us
  starting transfers between devices: 0.9 us -> 56.8 us
    reduce_scatter x7 -> x0, waiting for transfers between devices: 778 us -> none  [the longest x1 154 us: per_device(): lax.psum_scatter(totals[5], ('dp', 'seq'), scatter_dimension=0, tiled=True)]
    dot_general x70 -> x0, matrix products: 415 us -> none  [the longest x2 26.8 us: per_device(): jnp.einsum('td,fd->tf', upstream, down_full, preferred_element_type=jnp.f...]
    pallas_call x0 -> x13, Pallas kernels: none -> 216 us  [the longest x3 67.9 us: forward_group(): pl.pallas_call(forward_kernel, grid=(cols // TILE,), out_shape=(sds((toke...]
    ppermute x0 -> x59, waiting for transfers between devices: none -> 161 us  [the longest x20 90.7 us: reduce_rows(): came = lax.ppermute(send, AXES, stage_pairs(dp, bits, stage))]
    all_gather x6 -> x0, blocking collectives: 98.4 us -> none  [the longest x1 42 us: per_device(): lax.all_gather(w_key, ('dp', 'seq'), axis=0, tiled=True)]
    unnamed x2 -> x0, blocking collectives: 82.3 us -> none
    all_gather x9 -> x0, waiting for transfers between devices: 65.2 us -> none  [the longest x1 60 us: per_device(): lax.all_gather(w_down, ('dp', 'seq'), axis=1, tiled=True)]
    ppermute x0 -> x59, starting transfers between devices: none -> 56.8 us  [the longest x20 28.8 us: gather(): came = lax.ppermute(held, AXES, stage_pairs(dp, bits, stage))]
  transfers between devices with their start and end apart: 16 -> 59, of which waited for: 8 -> 21; matrix products, arithmetic and copies ran while one was open for 28% -> 7% of each run, Pallas kernels for 0% -> 41%
where the time goes in v1:
time: 527 us; the launch traced here: 522 us
  Pallas kernels  216 us (41%)
  waiting for transfers between devices  161 us (31%)
  local copies, waits for them, and re-layouts  60.1 us (11%)
  starting transfers between devices  56.8 us (11%)
  other arithmetic  26.1 us (5%)
    ppermute x20, waiting for transfers between devices, reduce_rows(): came = lax.ppermute(send, AXES, stage_pairs(dp, bits, stage))  90.7 us
    ppermute x20, waiting for transfers between devices, gather(): came = lax.ppermute(held, AXES, stage_pairs(dp, bits, stage))  69.8 us
    pallas_call x3, Pallas kernels, forward_group(): pl.pallas_call(forward_kernel, grid=(cols // TILE,), out_shape=(sds((toke...  67.9 us
    unnamed x169, local copies, waits for them, and re-layouts  46.3 us
    pallas_call x1, Pallas kernels, attend_back(): pl.pallas_call(functools.partial(attend_back_kernel, rows, count), grid=(...  38.7 us
    ppermute x20, starting transfers between devices, gather(): came = lax.ppermute(held, AXES, stage_pairs(dp, bits, stage))  28.8 us
    pallas_call x1, Pallas kernels, back(): pl.pallas_call(functools.partial(back_kernel, groups, rows, count), grid=...  27.1 us
    ppermute x20, starting transfers between devices, reduce_rows(): came = lax.ppermute(send, AXES, stage_pairs(dp, bits, stage))  23 us
  transfers between devices with their start and end apart: 59, of which 21 were waited for; matrix products, arithmetic and copies ran while one was open for 7% of the time, Pallas kernels for 41%

profile of v1, /device:TPU:0, one launch (start us, length us, event | category | flops | bytes accessed | tf_op | source)
XLA Modules:
  0.0 521.7 jit_solution(17448386107812626287)
XLA Ops:
  2.3 4.1 collective-permute-start.2
  8.7 2.9 collective-permute-start.14
  11.7 2.9 collective-permute-start.26
  14.6 12.3 %collective-permute-done.8 = bf16[32,1024]{1,0:T(8,128)(2,1)S(1)} collective-permute-done((bf16[32,1024]{1,0:T(8,128)(2,1)}, bf16[32,1024]{1,0:T(8,128)(2,1)S(1)}, u32[]{:S(2)}, u32[]{:S(2)}) %collective-permute-start.8) | collective-permute-done | bytes 65568 | tf_op jit(solution)/shard_map/ppermute | solution.py:93
  27.1 2.0 collective-permute-start.3
  29.1 8.6 %collective-permute-done.26 = bf16[3,32,768]{2,1,0:T(8,128)(2,1)S(1)} collective-permute-done((bf16[3,32,768]{2,1,0:T(8,128)(2,1)S(1)}, bf16[3,32,768]{2,1,0:T(8,128)(2,1)S(1)}, u32[]{:S(2)}, u32[]{:S(2)}) %collective-permute-start.26) | collective-permute-done | bytes 147488 | tf_op jit(solution)/shard_map/ppermute | solution.py:93
  38.5 2.0 collective-permute-done.9
  42.4 2.1 collective-permute-start.21
  48.7 11.1 %collective-permute-done.15 = bf16[3,64,1024]{2,1,0:T(8,128)(2,1)S(1)} collective-permute-done((bf16[3,64,1024]{2,1,0:T(8,128)(2,1)S(1)}, bf16[3,64,1024]{2,1,0:T(8,128)(2,1)S(1)}, u32[]{:S(2)}, u32[]{:S(2)}) %collective-permute-start.15) | collective-permute-done | bytes 393248 | tf_op jit(solution)/shard_map/ppermute | solution.py:93
  60.5 7.7 %collective-permute-done.21 = bf16[3,64,1024]{2,1,0:T(8,128)(2,1)S(1)} collective-permute-done((bf16[3,64,1024]{2,1,0:T(8,128)(2,1)S(1)}, bf16[3,64,1024]{2,1,0:T(8,128)(2,1)S(1)}, u32[]{:S(2)}, u32[]{:S(2)}) %collective-permute-start.21) | collective-permute-done | bytes 393248 | tf_op jit(solution)/shard_map/ppermute | solution.py:93
  76.4 19.2 %collective-permute-done.28 = bf16[3,128,768]{2,1,0:T(8,128)(2,1)S(1)} collective-permute-done((bf16[3,128,768]{2,1,0:T(8,128)(2,1)S(1)}, bf16[3,128,768]{2,1,0:T(8,128)(2,1)S(1)}, u32[]{:S(2)}, u32[]{:S(2)}) %collective-permute-start.28) | collective-permute-done | bytes 589856 | tf_op jit(solution)/shard_map/ppermute | solution.py:93
  100.0 7.9 %collective-permute-done.22 = bf16[3,128,1024]{2,1,0:T(8,128)(2,1)S(1)} collective-permute-done((bf16[3,128,1024]{2,1,0:T(8,128)(2,1)S(1)}, bf16[3,128,1024]{2,1,0:T(8,128)(2,1)S(1)}, u32[]{:S(2)}, u32[]{:S(2)}) %collective-permute-start.22) | collective-permute-done | bytes 786464 | tf_op jit(solution)/shard_map/ppermute | solution.py:93
  117.9 4.5 pre.1
  127.4 6.9 %project.1 = (bf16[1024,1024]{1,0:T(8,128)(2,1)S(1)}, bf16[1536,1024]{1,0:T(8,128)(2,1)S(1)}) custom-call(bf16[1024,1024]{1,0:T(8,128)(2,1)S(1)} %get-tuple-element.48.xt, f32[1,1024]{1,0:T(1,128)S(1)} %get-tuple-element.49.r1, bf16[256,1664]{1,0:T(8,128)(2,1)} %pad_maximum_fusion.4.w0, bf16[256,1664]{1,0:T(8,128)(2,1)} %collective-permute-done.5.w1, ...), custom_call_target="tpu_custom_call" | custom-call | flops 3221225472 | bytes 10485760 | tf_op jit(solution)/shard_map/project/pallas_call | solution.py:184
  137.9 20.6 %attend.1 = (bf16[1024,1024]{1,0:T(8,128)(2,1)S(1)}, f32[16,1,1024]{2,1,0:T(1,128)S(1)}) custom-call(s32[72]{0:T(128)S(1)} %pad_add_fusion.tab, bf16[1536,1024]{1,0:T(8,128)(2,1)S(1)} %get-tuple-element.50.q.k.v, bf16[1536,1024]{1,0:T(8,128)(2,1)S(1)} %get-tuple-element.50.q.k.v, bf16[1536,1024]{1,0:T(8,128)(2,1)S(1)} %get-tuple-element.50.q.k.v), custom_call_target="tpu_custom_call" | custom-call | flops 8589934592 | bytes 8388608 | tf_op jit(solution)/shard_map/attend/pallas_call | solution.py:241
  159.8 1.7 copy-done.46
  162.6 10.3 %middle.1 = (f32[1024,1024]{1,0:T(8,128)}, f32[1,1024]{1,0:T(1,128)S(1)}, bf16[1024,1024]{1,0:T(8,128)(2,1)S(1)}, bf16[1024,1024]{1,0:T(8,128)(2,1)}) custom-call(s32[72]{0:T(128)S(1)} %pad_add_fusion.tab, bf16[1024,1024]{1,0:T(8,128)(2,1)} %copy-done.42, bf16[256,1024]{1,0:T(8,128)(2,1)S(1)} %copy-done.29, bf16[256,1024]{1,0:T(8,128)(2,1)S(1)} %copy-done.34, ...), custom_call_target="tpu_custom_call" | custom-call | flops 2147483648 | bytes 16777216 | tf_op jit(solution)/shard_map/middle/pallas_call | solution.py:293
  177.4 17.8 %forward_group.5 = (bf16[1024,768]{1,0:T(8,128)(2,1)S(1)}, bf16[1024,768]{1,0:T(8,128)(2,1)S(1)}, bf16[1024,768]{1,0:T(8,128)(2,1)S(1)}, bf16[3,512,768]{2,1,0:T(8,128)(2,1)}, bf16[3,512,768]{2,1,0:T(8,128)(2,1)}) custom-call(bf16[1024,1024]{1,0:T(8,128)(2,1)S(1)} %copy-done.45, bf16[1024,1024]{1,0:T(8,128)(2,1)S(1)} %get-tuple-element.53.x2t, ...), custom_call_target="tpu_custom_call" | custom-call | flops 9663676416 | bytes 22544384 | tf_op jit(solution)/shard_map/forward_group/pallas_call | solution.py:342
  200.6 25.1 %forward_group.3 = (bf16[1024,1024]{1,0:T(8,128)(2,1)S(1)}, bf16[1024,1024]{1,0:T(8,128)(2,1)S(1)}, bf16[1024,1024]{1,0:T(8,128)(2,1)S(1)}, bf16[3,512,1024]{2,1,0:T(8,128)(2,1)}, bf16[3,512,1024]{2,1,0:T(8,128)(2,1)}) custom-call(bf16[1024,1024]{1,0:T(8,128)(2,1)} %get-tuple-element.52.x2, bf16[1024,1024]{1,0:T(8,128)(2,1)} %copy-done.44, ...), custom_call_target="tpu_custom_call" | custom-call | flops 12884901888 | bytes 27262976 | tf_op jit(solution)/shard_map/forward_group/pallas_call | solution.py:342
  229.7 25.0 %forward_group.4 = (bf16[1024,1024]{1,0:T(8,128)(2,1)S(1)}, bf16[1024,1024]{1,0:T(8,128)(2,1)S(1)}, bf16[1024,1024]{1,0:T(8,128)(2,1)S(1)}, bf16[3,512,1024]{2,1,0:T(8,128)(2,1)}, bf16[3,512,1024]{2,1,0:T(8,128)(2,1)}) custom-call(bf16[1024,1024]{1,0:T(8,128)(2,1)} %get-tuple-element.52.x2, bf16[1024,1024]{1,0:T(8,128)(2,1)} %copy-done.44, ...), custom_call_target="tpu_custom_call" | custom-call | flops 12884901888 | bytes 27262976 | tf_op jit(solution)/shard_map/forward_group/pallas_call | solution.py:342
  258.7 27.1 %back.1 = (f32[1024,1024]{1,0:T(8,128)}, bf16[1024,1024]{1,0:T(8,128)(2,1)}) custom-call(s32[72]{0:T(128)S(1)} %pad_add_fusion.tab, bf16[1024,1024]{1,0:T(8,128)(2,1)} %copy-done.52, bf16[1024,1024]{1,0:T(8,128)(2,1)} %copy-done.53, bf16[1024,1024]{1,0:T(8,128)(2,1)} %copy-done.54, bf16[1024,1024]{1,0:T(8,128)(2,1)} %copy-done.55, ...), custom_call_target="tpu_custom_call" | custom-call | flops 11811160064 | bytes 39845888 | tf_op jit(solution)/shard_map/back/pallas_call | solution.py:435
  287.5 6.3 %mixed.1 = (bf16[512,1024]{1,0:T(8,128)(2,1)}, bf16[512,1024]{1,0:T(8,128)(2,1)S(1)}, f32[1024,1024]{1,0:T(8,128)S(1)}) custom-call(bf16[1024,1024]{1,0:T(8,128)(2,1)S(1)} %copy-done.56, bf16[1024,1024]{1,0:T(8,128)(2,1)S(1)} %copy-done.43, bf16[256,1024]{1,0:T(8,128)(2,1)S(1)} %copy-done.30, bf16[256,1024]{1,0:T(8,128)(2,1)S(1)} %copy-done.35, ...), custom_call_target="tpu_custom_call" | custom-call | flops 4294967296 | bytes 12582912 | tf_op jit(solution)/shard_map/mixed/pallas_call | solution.py:516
  294.9 2.1 copy-done.50
  297.0 2.2 copy-done.51
  299.2 38.7 %attend_back.1 = (bf16[256,1024]{1,0:T(8,128)(2,1)S(1)}, bf16[256,1024]{1,0:T(8,128)(2,1)S(1)}, bf16[1024,1024]{1,0:T(8,128)(2,1)S(1)}) custom-call(s32[72]{0:T(128)S(1)} %pad_add_fusion.tab, bf16[1536,1024]{1,0:T(8,128)(2,1)S(1)} %copy-done.47, bf16[1536,1024]{1,0:T(8,128)(2,1)S(1)} %copy-done.47, bf16[1536,1024]{1,0:T(8,128)(2,1)S(1)} %copy-done.47, ...), custom_call_target="tpu_custom_call" | custom-call | flops 25769803776 | bytes 16777216 | tf_op jit(solution)/shard_map/attend_back/pallas_call | solution.py:580
  337.9 4.7 weights_of.1
  343.0 11.4 %input_of.1 = bf16[1024,1024]{1,0:T(8,128)(2,1)} custom-call(s32[72]{0:T(128)S(1)} %pad_add_fusion.tab, bf16[256,1024]{1,0:T(8,128)(2,1)S(1)} %get-tuple-element.70.dq, bf16[256,1024]{1,0:T(8,128)(2,1)S(1)} %get-tuple-element.71.dk, bf16[1024,1024]{1,0:T(8,128)(2,1)} %copy-done.9, bf16[256,1664]{1,0:T(8,128)(2,1)} %pad_maximum_fusion.4.w0, ...), custom_call_target="tpu_custom_call" | custom-call | flops 3221225472 | bytes 15728640 | tf_op jit(solution)/shard_map/input_of/pallas_call | solution.py:662
  354.4 3.2 dynamic-slice_bitcast_fusion
  358.1 2.1 add_convert_fusion.15
  366.4 17.8 %output_of.1 = bf16[1024,1024]{1,0:T(8,128)(2,1)} custom-call(s32[72]{0:T(128)S(1)} %pad_add_fusion.tab, bf16[1024,1024]{1,0:T(8,128)(2,1)} %copy-done.10, bf16[1024,1024]{1,0:T(8,128)(2,1)} %copy-done.11, bf16[1024,768]{1,0:T(8,128)(2,1)S(1)} %copy-done.19, bf16[3,256,1024]{2,1,0:T(8,128)(2,1)S(1)} %copy-done.1, ...), custom_call_target="tpu_custom_call" | custom-call | flops 5905580032 | bytes 17825792 | tf_op jit(solution)/shard_map/output_of/pallas_call | solution.py:484
  384.3 1.9 dynamic-slice_bitcast_fusion.1
  387.3 3.2 maximum_select_fusion.1
  392.0 1.9 add_convert_fusion.11
  395.5 2.2 add_convert_fusion.5
  400.8 3.3 collective-permute-done.42
  404.1 2.1 collective-permute-start.43
  406.4 2.1 collective-permute-start.36
  408.5 14.3 %collective-permute-done.55 = bf16[3,256,768]{2,1,0:T(8,128)(2,1)S(1)} collective-permute-done((bf16[3,256,768]{2,1,0:T(8,128)(2,1)S(1)}, bf16[3,256,768]{2,1,0:T(8,128)(2,1)S(1)}, u32[]{:S(2)}, u32[]{:S(2)}) %collective-permute-start.55) | collective-permute-done | bytes 1179680 | tf_op jit(solution)/shard_map/ppermute | solution.py:112
  430.8 5.5 %collective-permute-done.37 = bf16[64,1536]{1,0:T(8,128)(2,1)S(1)} collective-permute-done((bf16[64,1536]{1,0:T(8,128)(2,1)S(1)}, bf16[64,1536]{1,0:T(8,128)(2,1)S(1)}, u32[]{:S(2)}, u32[]{:S(2)}) %collective-permute-start.37) | collective-permute-done | bytes 196640 | tf_op jit(solution)/shard_map/ppermute | solution.py:112
  436.4 2.4 collective-permute-start.38
  438.9 1.8 collective-permute-start.57
  442.6 6.4 %collective-permute-done.45 = bf16[3,256,1024]{2,1,0:T(8,128)(2,1)S(1)} collective-permute-done((bf16[3,256,1024]{2,1,0:T(8,128)(2,1)S(1)}, bf16[3,256,1024]{2,1,0:T(8,128)(2,1)S(1)}, u32[]{:S(2)}, u32[]{:S(2)}) %collective-permute-start.45) | collective-permute-done | bytes 1572896 | tf_op jit(solution)/shard_map/ppermute | solution.py:112
  450.7 23.6 %collective-permute-done.50 = bf16[3,256,1024]{2,1,0:T(8,128)(2,1)S(1)} collective-permute-done((bf16[3,256,1024]{2,1,0:T(8,128)(2,1)S(1)}, bf16[3,256,1024]{2,1,0:T(8,128)(2,1)S(1)}, u32[]{:S(2)}, u32[]{:S(2)}) %collective-permute-start.50) | collective-permute-done | bytes 1572896 | tf_op jit(solution)/shard_map/ppermute | solution.py:112
  479.8 2.6 collective-permute-start.47
  482.3 4.7 collective-permute-done.51
  488.7 5.9 %collective-permute-done.47 = bf16[3,64,1024]{2,1,0:T(8,128)(2,1)S(1)} collective-permute-done((bf16[3,64,1024]{2,1,0:T(8,128)(2,1)S(1)}, bf16[3,64,1024]{2,1,0:T(8,128)(2,1)S(1)}, u32[]{:S(2)}, u32[]{:S(2)}) %collective-permute-start.47) | collective-permute-done | bytes 393248 | tf_op jit(solution)/shard_map/ppermute | solution.py:112
  495.0 12.3 %collective-permute-done.52 = bf16[3,64,1024]{2,1,0:T(8,128)(2,1)S(1)} collective-permute-done((bf16[3,64,1024]{2,1,0:T(8,128)(2,1)S(1)}, bf16[3,64,1024]{2,1,0:T(8,128)(2,1)S(1)}, u32[]{:S(2)}, u32[]{:S(2)}) %collective-permute-start.52) | collective-permute-done | bytes 393248 | tf_op jit(solution)/shard_map/ppermute | solution.py:112
  507.7 11.3 %collective-permute-done.53 = bf16[3,32,1024]{2,1,0:T(8,128)(2,1)S(1)} collective-permute-done((bf16[3,32,1024]{2,1,0:T(8,128)(2,1)S(1)}, bf16[3,32,1024]{2,1,0:T(8,128)(2,1)S(1)}, u32[]{:S(2)}, u32[]{:S(2)}) %collective-permute-start.53) | collective-permute-done | bytes 196640 | tf_op jit(solution)/shard_map/ppermute | solution.py:112
  (322 shorter events, 102.2 us)
Async XLA Ops:
  2.3 24.8 %collective-permute-start.2 = (bf16[32,1664]{1,0:T(8,128)(2,1)S(1)}, bf16[32,1664]{1,0:T(8,128)(2,1)S(1)}, u32[]{:S(2)}, u32[]{:S(2)}) collective-permute-start(bf16[32,1664]{1,0:T(8,128)(2,1)S(1)} %pad_maximum_fusion.18), channel_id=1, source_target_pairs={{0,16},{1,17},{2,18},{3,19},{4,20},{5,21},{6,22},{7,23},{8,24},{9,... | collective-permute-start | bytes 319496 | tf_op jit(solution)/shard_map/ppermute | solution.py:93
  6.4 20.5 %collective-permute-start.8 = (bf16[32,1024]{1,0:T(8,128)(2,1)}, bf16[32,1024]{1,0:T(8,128)(2,1)S(1)}, u32[]{:S(2)}, u32[]{:S(2)}) collective-permute-start(bf16[32,1024]{1,0:T(8,128)(2,1)} %param.20), channel_id=1, source_target_pairs={{0,16},{1,17},{2,18},{3,19},{4,20},{5,21},{6,22},{7,23},{8,24},{9,... | collective-permute-start | bytes 196616 | tf_op jit(solution)/shard_map/ppermute | solution.py:93
  8.7 33.6 %collective-permute-start.14 = (bf16[3,32,1024]{2,1,0:T(8,128)(2,1)S(1)}, bf16[3,32,1024]{2,1,0:T(8,128)(2,1)S(1)}, u32[]{:S(2)}, u32[]{:S(2)}) collective-permute-start(bf16[3,32,1024]{2,1,0:T(8,128)(2,1)S(1)} %get-tuple-element.123), channel_id=1, source_target_pairs={{0,16},{1,17},{2,18},{3,19},{4,20},{5,21},{6,22},{7,23},{8,24},{9,... | collective-permute-start | bytes 589832 | tf_op jit(solution)/shard_map/ppermute | solution.py:93
  11.6 30.8 %collective-permute-start.20 = (bf16[3,32,1024]{2,1,0:T(8,128)(2,1)S(1)}, bf16[3,32,1024]{2,1,0:T(8,128)(2,1)S(1)}, u32[]{:S(2)}, u32[]{:S(2)}) collective-permute-start(bf16[3,32,1024]{2,1,0:T(8,128)(2,1)S(1)} %get-tuple-element.122), channel_id=1, source_target_pairs={{0,16},{1,17},{2,18},{3,19},{4,20},{5,21},{6,22},{7,23},{8,24},{9,... | collective-permute-start | bytes 589832 | tf_op jit(solution)/shard_map/ppermute | solution.py:93
  11.7 26.1 %collective-permute-start.26 = (bf16[3,32,768]{2,1,0:T(8,128)(2,1)S(1)}, bf16[3,32,768]{2,1,0:T(8,128)(2,1)S(1)}, u32[]{:S(2)}, u32[]{:S(2)}) collective-permute-start(bf16[3,32,768]{2,1,0:T(8,128)(2,1)S(1)} %pad_maximum_fusion.16), channel_id=1, source_target_pairs={{0,16},{1,17},{2,18},{3,19},{4,20},{5,21},{6,22},{7,23},{8,24},{9,... | collective-permute-start | bytes 442376 | tf_op jit(solution)/shard_map/ppermute | solution.py:93
  26.9 13.6 %collective-permute-start.9 = (bf16[64,1024]{1,0:T(8,128)(2,1)S(1)}, bf16[64,1024]{1,0:T(8,128)(2,1)S(1)}, u32[]{:S(2)}, u32[]{:S(2)}) collective-permute-start(bf16[64,1024]{1,0:T(8,128)(2,1)S(1)} %pad_maximum_fusion.17), channel_id=1, source_target_pairs={{0,8},{1,9},{2,10},{3,11},{4,12},{5,13},{6,14},{7,15},{8,0},{9,1},... | collective-permute-start | bytes 393224 | tf_op jit(solution)/shard_map/ppermute | solution.py:93
  27.1 18.0 %collective-permute-start.3 = (bf16[64,1664]{1,0:T(8,128)(2,1)S(1)}, bf16[64,1664]{1,0:T(8,128)(2,1)S(1)}, u32[]{:S(2)}, u32[]{:S(2)}) collective-permute-start(bf16[64,1664]{1,0:T(8,128)(2,1)S(1)} %pad_maximum_fusion.15), channel_id=1, source_target_pairs={{0,8},{1,9},{2,10},{3,11},{4,12},{5,13},{6,14},{7,15},{8,0},{9,1},... | collective-permute-start | bytes 638984 | tf_op jit(solution)/shard_map/ppermute | solution.py:93
  37.8 22.2 %collective-permute-start.27 = (bf16[3,64,768]{2,1,0:T(8,128)(2,1)S(1)}, bf16[3,64,768]{2,1,0:T(8,128)(2,1)S(1)}, u32[]{:S(2)}, u32[]{:S(2)}) collective-permute-start(bf16[3,64,768]{2,1,0:T(8,128)(2,1)S(1)} %pad_maximum_fusion.12), channel_id=1, source_target_pairs={{0,8},{1,9},{2,10},{3,11},{4,12},{5,13},{6,14},{7,15},{8,0},{9,1},... | collective-permute-start | bytes 884744 | tf_op jit(solution)/shard_map/ppermute | solution.py:93
  42.3 17.6 %collective-permute-start.15 = (bf16[3,64,1024]{2,1,0:T(8,128)(2,1)S(1)}, bf16[3,64,1024]{2,1,0:T(8,128)(2,1)S(1)}, u32[]{:S(2)}, u32[]{:S(2)}) collective-permute-start(bf16[3,64,1024]{2,1,0:T(8,128)(2,1)S(1)} %pad_maximum_fusion.10), channel_id=1, source_target_pairs={{0,8},{1,9},{2,10},{3,11},{4,12},{5,13},{6,14},{7,15},{8,0},{9,1},... | collective-permute-start | bytes 1179656 | tf_op jit(solution)/shard_map/ppermute | solution.py:93
  42.4 25.8 %collective-permute-start.21 = (bf16[3,64,1024]{2,1,0:T(8,128)(2,1)S(1)}, bf16[3,64,1024]{2,1,0:T(8,128)(2,1)S(1)}, u32[]{:S(2)}, u32[]{:S(2)}) collective-permute-start(bf16[3,64,1024]{2,1,0:T(8,128)(2,1)S(1)} %pad_maximum_fusion.11), channel_id=1, source_target_pairs={{0,8},{1,9},{2,10},{3,11},{4,12},{5,13},{6,14},{7,15},{8,0},{9,1},... | collective-permute-start | bytes 1179656 | tf_op jit(solution)/shard_map/ppermute | solution.py:93
  45.1 24.7 %collective-permute-start.4 = (bf16[128,1664]{1,0:T(8,128)(2,1)S(1)}, bf16[128,1664]{1,0:T(8,128)(2,1)S(1)}, u32[]{:S(2)}, u32[]{:S(2)}) collective-permute-start(bf16[128,1664]{1,0:T(8,128)(2,1)S(1)} %pad_maximum_fusion.9), channel_id=1, source_target_pairs={{0,4},{1,3},{2,6},{3,1},{4,0},{5,7},{6,2},{7,5},{8,12},{9,11},{10,... | collective-permute-start | bytes 1277960 | tf_op jit(solution)/shard_map/ppermute | solution.py:93
  47.0 23.4 %collective-permute-start.11 = (bf16[256,1024]{1,0:T(8,128)(2,1)S(1)}, bf16[256,1024]{1,0:T(8,128)(2,1)S(1)}, u32[]{:S(2)}, u32[]{:S(2)}) collective-permute-start(bf16[256,1024]{1,0:T(8,128)(2,1)S(1)} %constant_dynamic-update-slice_fusion.w0), channel_id=1, source_target_pairs={{0,2},{1,5},{2,0},{3,7},{4,6},{5,1},{6,4},{7,3},{8,10},{9,13},{10,... | collective-permute-start | bytes 1572872 | tf_op jit(solution)/shard_map/ppermute | solution.py:93
  59.8 14.0 %collective-permute-start.12 = (bf16[256,1024]{1,0:T(8,128)(2,1)S(1)}, bf16[256,1024]{1,0:T(8,128)(2,1)S(1)}, u32[]{:S(2)}, u32[]{:S(2)}) collective-permute-start(bf16[256,1024]{1,0:T(8,128)(2,1)S(1)} %constant_dynamic-update-slice_fusion.w0), channel_id=1, source_target_pairs={{0,1},{1,0},{2,3},{3,2},{4,5},{5,4},{6,7},{7,6},{8,9},{9,8},{10,11... | collective-permute-start | bytes 1572872 | tf_op jit(solution)/shard_map/ppermute | solution.py:97
  59.9 38.6 %collective-permute-start = (bf16[512,1024]{1,0:T(8,128)(2,1)S(1)}, bf16[512,1024]{1,0:T(8,128)(2,1)S(1)}, u32[]{:S(2)}, u32[]{:S(2)}) collective-permute-start(bf16[512,1024]{1,0:T(8,128)(2,1)S(1)} %dynamic-slice_bitcast_fusion.3), channel_id=1, source_target_pairs={{0,1},{1,0},{2,3},{3,2},{4,5},{5,4},{6,7},{7,6},{8,9},{9,8},{10,11... | collective-permute-start | bytes 3145736 | tf_op jit(solution)/shard_map/ppermute | solution.py:700
  68.2 28.6 %collective-permute-start.16 = (bf16[3,128,1024]{2,1,0:T(8,128)(2,1)S(1)}, bf16[3,128,1024]{2,1,0:T(8,128)(2,1)S(1)}, u32[]{:S(2)}, u32[]{:S(2)}) collective-permute-start(bf16[3,128,1024]{2,1,0:T(8,128)(2,1)S(1)} %pad_maximum_fusion.5), channel_id=1, source_target_pairs={{0,4},{1,3},{2,6},{3,1},{4,0},{5,7},{6,2},{7,5},{8,12},{9,11},{10,... | collective-permute-start | bytes 2359304 | tf_op jit(solution)/shard_map/ppermute | solution.py:93
  69.8 25.8 %collective-permute-start.28 = (bf16[3,128,768]{2,1,0:T(8,128)(2,1)S(1)}, bf16[3,128,768]{2,1,0:T(8,128)(2,1)S(1)}, u32[]{:S(2)}, u32[]{:S(2)}) collective-permute-start(bf16[3,128,768]{2,1,0:T(8,128)(2,1)S(1)} %pad_maximum_fusion.7), channel_id=1, source_target_pairs={{0,4},{1,3},{2,6},{3,1},{4,0},{5,7},{6,2},{7,5},{8,12},{9,11},{10,... | collective-permute-start | bytes 1769480 | tf_op jit(solution)/shard_map/ppermute | solution.py:93
  71.2 36.7 %collective-permute-start.22 = (bf16[3,128,1024]{2,1,0:T(8,128)(2,1)S(1)}, bf16[3,128,1024]{2,1,0:T(8,128)(2,1)S(1)}, u32[]{:S(2)}, u32[]{:S(2)}) collective-permute-start(bf16[3,128,1024]{2,1,0:T(8,128)(2,1)S(1)} %pad_maximum_fusion.6), channel_id=1, source_target_pairs={{0,4},{1,3},{2,6},{3,1},{4,0},{5,7},{6,2},{7,5},{8,12},{9,11},{10,... | collective-permute-start | bytes 2359304 | tf_op jit(solution)/shard_map/ppermute | solution.py:93
  73.8 35.0 %collective-permute-start.5 = (bf16[256,1664]{1,0:T(8,128)(2,1)}, bf16[256,1664]{1,0:T(8,128)(2,1)}, u32[]{:S(2)}, u32[]{:S(2)}) collective-permute-start(bf16[256,1664]{1,0:T(8,128)(2,1)} %pad_maximum_fusion.4.w0), channel_id=1, source_target_pairs={{0,2},{1,5},{2,0},{3,7},{4,6},{5,1},{6,4},{7,3},{8,10},{9,13},{10,... | collective-permute-start | bytes 2555912 | tf_op jit(solution)/shard_map/ppermute | solution.py:93
  95.6 15.2 %collective-permute-start.1 = (bf16[512,1024]{1,0:T(8,128)(2,1)}, bf16[512,1024]{1,0:T(8,128)(2,1)}, u32[]{:S(2)}, u32[]{:S(2)}) collective-permute-start(bf16[512,1024]{1,0:T(8,128)(2,1)} %dynamic-slice_bitcast_fusion.2), channel_id=1, source_target_pairs={{0,1},{1,0},{2,3},{3,2},{4,5},{5,4},{6,7},{7,6},{8,9},{9,8},{10,11... | collective-permute-start | bytes 3145736 | tf_op jit(solution)/shard_map/ppermute | solution.py:701
  96.8 30.1 %collective-permute-start.29 = (bf16[3,256,768]{2,1,0:T(8,128)(2,1)}, bf16[3,256,768]{2,1,0:T(8,128)(2,1)}, u32[]{:S(2)}, u32[]{:S(2)}) collective-permute-start(bf16[3,256,768]{2,1,0:T(8,128)(2,1)} %pad_maximum_fusion.2.w0.refs_11_.refs_14_), channel_id=1, source_target_pairs={{0,2},{1,5},{2,0},{3,7},{4,6},{5,1},{6,4},{7,3},{8,10},{9,13},{10,... | collective-permute-start | bytes 3538952 | tf_op jit(solution)/shard_map/ppermute | solution.py:93
  99.5 38.3 %collective-permute-start.17 = (bf16[3,256,1024]{2,1,0:T(8,128)(2,1)S(1)}, bf16[3,256,1024]{2,1,0:T(8,128)(2,1)}, u32[]{:S(2)}, u32[]{:S(2)}) collective-permute-start(bf16[3,256,1024]{2,1,0:T(8,128)(2,1)S(1)} %pad_maximum_fusion.w0.refs_3_.refs_6_), channel_id=1, source_target_pairs={{0,2},{1,5},{2,0},{3,7},{4,6},{5,1},{6,4},{7,3},{8,10},{9,13},{10,... | collective-permute-start | bytes 4718600 | tf_op jit(solution)/shard_map/ppermute | solution.py:93
  108.9 18.5 %collective-permute-start.7 = (bf16[256,1664]{1,0:T(8,128)(2,1)}, bf16[256,1664]{1,0:T(8,128)(2,1)}, u32[]{:S(2)}, u32[]{:S(2)}) collective-permute-start(bf16[256,1664]{1,0:T(8,128)(2,1)} %collective-permute-done.5.w1), channel_id=1, source_target_pairs={{0,1},{1,0},{2,3},{3,2},{4,5},{5,4},{6,7},{7,6},{8,9},{9,8},{10,11... | collective-permute-start | bytes 2555912 | tf_op jit(solution)/shard_map/ppermute | solution.py:97
  110.8 62.6 %collective-permute-start.23 = (bf16[3,256,1024]{2,1,0:T(8,128)(2,1)S(1)}, bf16[3,256,1024]{2,1,0:T(8,128)(2,1)}, u32[]{:S(2)}, u32[]{:S(2)}) collective-permute-start(bf16[3,256,1024]{2,1,0:T(8,128)(2,1)S(1)} %pad_maximum_fusion.1.w0.refs_7_.refs_10_), channel_id=1, source_target_pairs={{0,2},{1,5},{2,0},{3,7},{4,6},{5,1},{6,4},{7,3},{8,10},{9,13},{10,... | collective-permute-start | bytes 4718600 | tf_op jit(solution)/shard_map/ppermute | solution.py:93
  112.5 24.0 %collective-permute-start.13 = (bf16[256,1024]{1,0:T(8,128)(2,1)}, bf16[256,1024]{1,0:T(8,128)(2,1)S(1)}, u32[]{:S(2)}, u32[]{:S(2)}) collective-permute-start(bf16[256,1024]{1,0:T(8,128)(2,1)} %copy-done.33), channel_id=1, source_target_pairs={{0,1},{1,0},{2,3},{3,2},{4,5},{5,4},{6,7},{7,6},{8,9},{9,8},{10,11... | collective-permute-start | bytes 1572872 | tf_op jit(solution)/shard_map/ppermute | solution.py:97
  126.8 46.1 %collective-permute-start.30 = (bf16[3,256,768]{2,1,0:T(8,128)(2,1)}, bf16[3,256,768]{2,1,0:T(8,128)(2,1)S(1)}, u32[]{:S(2)}, u32[]{:S(2)}) collective-permute-start(bf16[3,256,768]{2,1,0:T(8,128)(2,1)} %pad_maximum_fusion.2.w0.refs_11_.refs_14_), channel_id=1, source_target_pairs={{0,1},{1,0},{2,3},{3,2},{4,5},{5,4},{6,7},{7,6},{8,9},{9,8},{10,11... | collective-permute-start | bytes 3538952 | tf_op jit(solution)/shard_map/ppermute | solution.py:97
  127.3 46.2 %collective-permute-start.31 = (bf16[3,256,768]{2,1,0:T(8,128)(2,1)}, bf16[3,256,768]{2,1,0:T(8,128)(2,1)S(1)}, u32[]{:S(2)}, u32[]{:S(2)}) collective-permute-start(bf16[3,256,768]{2,1,0:T(8,128)(2,1)} %collective-permute-done.29.w1.refs_12_.refs_15_), channel_id=1, source_target_pairs={{0,1},{1,0},{2,3},{3,2},{4,5},{5,4},{6,7},{7,6},{8,9},{9,8},{10,11... | collective-permute-start | bytes 3538952 | tf_op jit(solution)/shard_map/ppermute | solution.py:97
  137.4 63.2 %collective-permute-start.18 = (bf16[3,256,1024]{2,1,0:T(8,128)(2,1)S(1)}, bf16[3,256,1024]{2,1,0:T(8,128)(2,1)S(1)}, u32[]{:S(2)}, u32[]{:S(2)}) collective-permute-start(bf16[3,256,1024]{2,1,0:T(8,128)(2,1)S(1)} %pad_maximum_fusion.w0.refs_3_.refs_6_), channel_id=1, source_target_pairs={{0,1},{1,0},{2,3},{3,2},{4,5},{5,4},{6,7},{7,6},{8,9},{9,8},{10,11... | collective-permute-start | bytes 4718600 | tf_op jit(solution)/shard_map/ppermute | solution.py:97
  137.8 62.8 %collective-permute-start.19 = (bf16[3,256,1024]{2,1,0:T(8,128)(2,1)}, bf16[3,256,1024]{2,1,0:T(8,128)(2,1)S(1)}, u32[]{:S(2)}, u32[]{:S(2)}) collective-permute-start(bf16[3,256,1024]{2,1,0:T(8,128)(2,1)} %collective-permute-done.17.w1.refs_4_.refs_7_), channel_id=1, source_target_pairs={{0,1},{1,0},{2,3},{3,2},{4,5},{5,4},{6,7},{7,6},{8,9},{9,8},{10,11... | collective-permute-start | bytes 4718600 | tf_op jit(solution)/shard_map/ppermute | solution.py:97
  173.0 56.7 %collective-permute-start.24 = (bf16[3,256,1024]{2,1,0:T(8,128)(2,1)S(1)}, bf16[3,256,1024]{2,1,0:T(8,128)(2,1)S(1)}, u32[]{:S(2)}, u32[]{:S(2)}) collective-permute-start(bf16[3,256,1024]{2,1,0:T(8,128)(2,1)S(1)} %pad_maximum_fusion.1.w0.refs_7_.refs_10_), channel_id=1, source_target_pairs={{0,1},{1,0},{2,3},{3,2},{4,5},{5,4},{6,7},{7,6},{8,9},{9,8},{10,11... | collective-permute-start | bytes 4718600 | tf_op jit(solution)/shard_map/ppermute | solution.py:97
  173.4 56.2 %collective-permute-start.25 = (bf16[3,256,1024]{2,1,0:T(8,128)(2,1)}, bf16[3,256,1024]{2,1,0:T(8,128)(2,1)S(1)}, u32[]{:S(2)}, u32[]{:S(2)}) collective-permute-start(bf16[3,256,1024]{2,1,0:T(8,128)(2,1)} %collective-permute-done.23.w1.refs_8_.refs_11_), channel_id=1, source_target_pairs={{0,1},{1,0},{2,3},{3,2},{4,5},{5,4},{6,7},{7,6},{8,9},{9,8},{10,11... | collective-permute-start | bytes 4718600 | tf_op jit(solution)/shard_map/ppermute | solution.py:97
  200.2 193.8 %collective-permute-start.54 = (bf16[3,512,768]{2,1,0:T(8,128)(2,1)}, bf16[3,512,768]{2,1,0:T(8,128)(2,1)}, u32[]{:S(2)}, u32[]{:S(2)}) collective-permute-start(bf16[3,512,768]{2,1,0:T(8,128)(2,1)} %get-tuple-element.84), channel_id=1, source_target_pairs={{0,1},{1,0},{2,3},{3,2},{4,5},{5,4},{6,7},{7,6},{8,9},{9,8},{10,11... | collective-permute-start | bytes 7077896 | tf_op jit(solution)/shard_map/ppermute | solution.py:101
  296.9 61.2 %collective-permute-start.39 = (bf16[512,1024]{1,0:T(8,128)(2,1)}, bf16[512,1024]{1,0:T(8,128)(2,1)}, u32[]{:S(2)}, u32[]{:S(2)}) collective-permute-start(bf16[512,1024]{1,0:T(8,128)(2,1)} %get-tuple-element.78), channel_id=1, source_target_pairs={{0,1},{1,0},{2,3},{3,2},{4,5},{5,4},{6,7},{7,6},{8,9},{9,8},{10,11... | collective-permute-start | bytes 3145736 | tf_op jit(solution)/shard_map/ppermute | solution.py:101
  342.6 48.3 %collective-permute-start.34 = (bf16[512,1536]{1,0:T(8,128)(2,1)}, bf16[512,1536]{1,0:T(8,128)(2,1)}, u32[]{:S(2)}, u32[]{:S(2)}) collective-permute-start(bf16[512,1536]{1,0:T(8,128)(2,1)} %get-tuple-element.76), channel_id=1, source_target_pairs={{0,1},{1,0},{2,3},{3,2},{4,5},{5,4},{6,7},{7,6},{8,9},{9,8},{10,11... | collective-permute-start | bytes 4718600 | tf_op jit(solution)/shard_map/ppermute | solution.py:101
  357.6 28.6 %collective-permute-start.33 = (bf16[512,1024]{1,0:T(8,128)(2,1)}, bf16[512,1024]{1,0:T(8,128)(2,1)}, u32[]{:S(2)}, u32[]{:S(2)}) collective-permute-start(bf16[512,1024]{1,0:T(8,128)(2,1)} %get-tuple-element.107), channel_id=1, source_target_pairs={{0,1},{1,0},{2,3},{3,2},{4,5},{5,4},{6,7},{7,6},{8,9},{9,8},{10,11... | collective-permute-start | bytes 3145736 | tf_op jit(solution)/shard_map/ppermute | solution.py:741
  357.7 66.6 %collective-permute-start.44 = (bf16[3,512,1024]{2,1,0:T(8,128)(2,1)}, bf16[3,512,1024]{2,1,0:T(8,128)(2,1)S(1)}, u32[]{:S(2)}, u32[]{:S(2)}) collective-permute-start(bf16[3,512,1024]{2,1,0:T(8,128)(2,1)} %get-tuple-element.80), channel_id=1, source_target_pairs={{0,1},{1,0},{2,3},{3,2},{4,5},{5,4},{6,7},{7,6},{8,9},{9,8},{10,11... | collective-permute-start | bytes 9437192 | tf_op jit(solution)/shard_map/ppermute | solution.py:101
  360.2 30.3 %collective-permute-start.40 = (bf16[256,1024]{1,0:T(8,128)(2,1)S(1)}, bf16[256,1024]{1,0:T(8,128)(2,1)S(1)}, u32[]{:S(2)}, u32[]{:S(2)}) collective-permute-start(bf16[256,1024]{1,0:T(8,128)(2,1)S(1)} %get-tuple-element.105), channel_id=1, source_target_pairs={{0,2},{1,5},{2,0},{3,7},{4,6},{5,1},{6,4},{7,3},{8,10},{9,13},{10,... | collective-permute-start | bytes 1572872 | tf_op jit(solution)/shard_map/ppermute | solution.py:112
  386.8 41.0 %collective-permute-start.49 = (bf16[3,512,1024]{2,1,0:T(8,128)(2,1)S(1)}, bf16[3,512,1024]{2,1,0:T(8,128)(2,1)S(1)}, u32[]{:S(2)}, u32[]{:S(2)}) collective-permute-start(bf16[3,512,1024]{2,1,0:T(8,128)(2,1)S(1)} %copy-done.80), channel_id=1, source_target_pairs={{0,1},{1,0},{2,3},{3,2},{4,5},{5,4},{6,7},{7,6},{8,9},{9,8},{10,11... | collective-permute-start | bytes 9437192 | tf_op jit(solution)/shard_map/ppermute | solution.py:101
  398.2 24.6 %collective-permute-start.55 = (bf16[3,256,768]{2,1,0:T(8,128)(2,1)S(1)}, bf16[3,256,768]{2,1,0:T(8,128)(2,1)S(1)}, u32[]{:S(2)}, u32[]{:S(2)}) collective-permute-start(bf16[3,256,768]{2,1,0:T(8,128)(2,1)S(1)} %get-tuple-element.95), channel_id=1, source_target_pairs={{0,2},{1,5},{2,0},{3,7},{4,6},{5,1},{6,4},{7,3},{8,10},{9,13},{10,... | collective-permute-start | bytes 3538952 | tf_op jit(solution)/shard_map/ppermute | solution.py:112
  404.1 26.0 %collective-permute-start.43 = (bf16[32,1024]{1,0:T(8,128)(2,1)S(1)}, bf16[32,1024]{1,0:T(8,128)(2,1)S(1)}, u32[]{:S(2)}, u32[]{:S(2)}) collective-permute-start(bf16[32,1024]{1,0:T(8,128)(2,1)S(1)} %add_convert_fusion.38), channel_id=1, source_target_pairs={{0,16},{1,17},{2,18},{3,19},{4,20},{5,21},{6,22},{7,23},{8,24},{9,... | collective-permute-start | bytes 196616 | tf_op jit(solution)/shard_map/ppermute | solution.py:112
  406.4 23.5 %collective-permute-start.36 = (bf16[128,1536]{1,0:T(8,128)(2,1)S(1)}, bf16[128,1536]{1,0:T(8,128)(2,1)S(1)}, u32[]{:S(2)}, u32[]{:S(2)}) collective-permute-start(bf16[128,1536]{1,0:T(8,128)(2,1)S(1)} %get-tuple-element.115), channel_id=1, source_target_pairs={{0,4},{1,3},{2,6},{3,1},{4,0},{5,7},{6,2},{7,5},{8,12},{9,11},{10,... | collective-permute-start | bytes 1179656 | tf_op jit(solution)/shard_map/ppermute | solution.py:112
  423.1 15.6 %collective-permute-start.56 = (bf16[3,128,768]{2,1,0:T(8,128)(2,1)S(1)}, bf16[3,128,768]{2,1,0:T(8,128)(2,1)S(1)}, u32[]{:S(2)}, u32[]{:S(2)}) collective-permute-start(bf16[3,128,768]{2,1,0:T(8,128)(2,1)S(1)} %get-tuple-element.103), channel_id=1, source_target_pairs={{0,4},{1,3},{2,6},{3,1},{4,0},{5,7},{6,2},{7,5},{8,12},{9,11},{10,... | collective-permute-start | bytes 1769480 | tf_op jit(solution)/shard_map/ppermute | solution.py:112
  426.3 22.7 %collective-permute-start.45 = (bf16[3,256,1024]{2,1,0:T(8,128)(2,1)S(1)}, bf16[3,256,1024]{2,1,0:T(8,128)(2,1)S(1)}, u32[]{:S(2)}, u32[]{:S(2)}) collective-permute-start(bf16[3,256,1024]{2,1,0:T(8,128)(2,1)S(1)} %get-tuple-element.91), channel_id=1, source_target_pairs={{0,2},{1,5},{2,0},{3,7},{4,6},{5,1},{6,4},{7,3},{8,10},{9,13},{10,... | collective-permute-start | bytes 4718600 | tf_op jit(solution)/shard_map/ppermute | solution.py:112
  429.4 44.9 %collective-permute-start.50 = (bf16[3,256,1024]{2,1,0:T(8,128)(2,1)S(1)}, bf16[3,256,1024]{2,1,0:T(8,128)(2,1)S(1)}, u32[]{:S(2)}, u32[]{:S(2)}) collective-permute-start(bf16[3,256,1024]{2,1,0:T(8,128)(2,1)S(1)} %get-tuple-element.93), channel_id=1, source_target_pairs={{0,2},{1,5},{2,0},{3,7},{4,6},{5,1},{6,4},{7,3},{8,10},{9,13},{10,... | collective-permute-start | bytes 4718600 | tf_op jit(solution)/shard_map/ppermute | solution.py:112
  438.9 38.9 %collective-permute-start.57 = (bf16[3,64,768]{2,1,0:T(8,128)(2,1)S(1)}, bf16[3,64,768]{2,1,0:T(8,128)(2,1)S(1)}, u32[]{:S(2)}, u32[]{:S(2)}) collective-permute-start(bf16[3,64,768]{2,1,0:T(8,128)(2,1)S(1)} %get-tuple-element.117), channel_id=1, source_target_pairs={{0,8},{1,9},{2,10},{3,11},{4,12},{5,13},{6,14},{7,15},{8,0},{9,1},... | collective-permute-start | bytes 884744 | tf_op jit(solution)/shard_map/ppermute | solution.py:112
  449.6 29.8 %collective-permute-start.46 = (bf16[3,128,1024]{2,1,0:T(8,128)(2,1)S(1)}, bf16[3,128,1024]{2,1,0:T(8,128)(2,1)S(1)}, u32[]{:S(2)}, u32[]{:S(2)}) collective-permute-start(bf16[3,128,1024]{2,1,0:T(8,128)(2,1)S(1)} %get-tuple-element.97), channel_id=1, source_target_pairs={{0,4},{1,3},{2,6},{3,1},{4,0},{5,7},{6,2},{7,5},{8,12},{9,11},{10,... | collective-permute-start | bytes 2359304 | tf_op jit(solution)/shard_map/ppermute | solution.py:112
  479.8 14.9 %collective-permute-start.47 = (bf16[3,64,1024]{2,1,0:T(8,128)(2,1)S(1)}, bf16[3,64,1024]{2,1,0:T(8,128)(2,1)S(1)}, u32[]{:S(2)}, u32[]{:S(2)}) collective-permute-start(bf16[3,64,1024]{2,1,0:T(8,128)(2,1)S(1)} %get-tuple-element.111), channel_id=1, source_target_pairs={{0,8},{1,9},{2,10},{3,11},{4,12},{5,13},{6,14},{7,15},{8,0},{9,1},... | collective-permute-start | bytes 1179656 | tf_op jit(solution)/shard_map/ppermute | solution.py:112
  487.3 20.0 %collective-permute-start.52 = (bf16[3,64,1024]{2,1,0:T(8,128)(2,1)S(1)}, bf16[3,64,1024]{2,1,0:T(8,128)(2,1)S(1)}, u32[]{:S(2)}, u32[]{:S(2)}) collective-permute-start(bf16[3,64,1024]{2,1,0:T(8,128)(2,1)S(1)} %get-tuple-element.113), channel_id=1, source_target_pairs={{0,8},{1,9},{2,10},{3,11},{4,12},{5,13},{6,14},{7,15},{8,0},{9,1},... | collective-permute-start | bytes 1179656 | tf_op jit(solution)/shard_map/ppermute | solution.py:112
  494.7 12.9 %collective-permute-start.48 = (bf16[3,32,1024]{2,1,0:T(8,128)(2,1)S(1)}, bf16[3,32,1024]{2,1,0:T(8,128)(2,1)S(1)}, u32[]{:S(2)}, u32[]{:S(2)}) collective-permute-start(bf16[3,32,1024]{2,1,0:T(8,128)(2,1)S(1)} %add_convert_fusion.28), channel_id=1, source_target_pairs={{0,16},{1,17},{2,18},{3,19},{4,20},{5,21},{6,22},{7,23},{8,24},{9,... | collective-permute-start | bytes 589832 | tf_op jit(solution)/shard_map/ppermute | solution.py:112
  (94 other events, 974.5 us)
